TPU v7x, 128 devices: a whole 4x4x4 slice. The times are simulated.
128 devices in a mesh: rep: 2 (over core), exp: 64 (over y, z, x).
Axes of the slice: x: 4, y: 4, z: 4, core: 2. Of those that a mesh axis runs over, the one named last changes fastest.
Arguments:
- tokens: bfloat16 [16384, 4096], P(('rep', 'exp')), may hold values from -6 to 6
- expert_ids: int32 [16384, 8], P(('rep', 'exp')), may hold values from 0 to 63, all different within a row; in each aligned block of 128 rows (0 to 127, 128 to 255, ...) at most 18 rows name the same one
- route_weights: bfloat16 [16384, 8], P(('rep', 'exp')), may hold values from 0.099609375 to 1
- cotangent: bfloat16 [16384, 4096], P(('rep', 'exp')), may hold values from -0.3984375 to 0.3984375
- w_gate: bfloat16 [64, 4096, 768], P('exp'), may hold values from -0.09375 to 0.09375
- w_up: bfloat16 [64, 4096, 768], P('exp'), may hold values from -0.09375 to 0.09375
- w_down: bfloat16 [64, 768, 4096], P('exp'), may hold values from -0.21875 to 0.21875
- ia3_scale: float32 [64, 768], P('exp'), may hold values from 0.25 to 1.75
Outputs:
- mixed: bfloat16 [16384, 4096], P(('rep', 'exp'))
- ia3_grad: float32 [64, 768], P('exp')
Inputs may be any that keep to these rules, and one draw needn't show every extreme that they name: `expert_ids`: among the choices of one device's 128 tokens, no expert is named more than 18 times, a bound that some block reaches; a token names 8 different experts.
All inputs are finite; a program needn't handle non-finite values.
Results may differ from a plain program's by a relative error of at most 0.0057.
Values may be sent and summed in bfloat16 or wider, within the bound.
A program may use at most 192 MiB of HBM per device.

v0:
```python
import jax
import jax.numpy as jnp
from jax import lax
from jax.sharding import PartitionSpec as P


def shards(tokens, expert_ids, route_weights, cotangent, w_gate, w_up, w_down, ia3_scale):
    owners = lax.axis_size("exp")
    tok_rows, model_width = tokens.shape
    per_token = expert_ids.shape[1]
    capacity = tok_rows * per_token // owners + tok_rows * per_token // (8 * owners)
    flat_ids = expert_ids.reshape(-1)
    one_hot = (flat_ids[:, None] == jnp.arange(owners, dtype=jnp.int32)[None, :]).astype(jnp.int32)
    before = jnp.cumsum(one_hot, axis=0) - one_hot
    slot_index = jnp.sum(before * one_hot, axis=1)
    source_row = jnp.arange(tok_rows * per_token, dtype=jnp.int32) // per_token

    def into_slots(values):
        empty = jnp.zeros((owners, capacity) + values.shape[1:], values.dtype)
        return empty.at[flat_ids, slot_index].set(values)

    token_send = into_slots(tokens[source_row])
    weight_send = into_slots(route_weights.reshape(-1))
    token_recv, weight_recv = (
        lax.all_to_all(token_send, "exp", split_axis=0, concat_axis=0, tiled=True),
        lax.all_to_all(weight_send, "exp", split_axis=0, concat_axis=0, tiled=True),
    )
    received_rows = token_recv.reshape(-1, model_width)
    gate_pre = jnp.dot(received_rows, w_gate[0], preferred_element_type=jnp.float32)
    up_pre = jnp.dot(received_rows, w_up[0], preferred_element_type=jnp.float32)
    activated = jax.nn.silu(gate_pre) * up_pre
    hidden = (ia3_scale[0][None, :] * activated).astype(jnp.bfloat16)
    expert_out = jnp.dot(hidden, w_down[0], preferred_element_type=jnp.float32).astype(jnp.bfloat16)
    returned = lax.all_to_all(
        expert_out.reshape(owners, capacity, model_width),
        "exp",
        split_axis=0,
        concat_axis=0,
        tiled=True,
    )
    picked = returned[flat_ids, slot_index].reshape(tok_rows, per_token, model_width)
    mixed = jnp.einsum(
        "tkd,tk->td", picked, route_weights, preferred_element_type=jnp.float32
    ).astype(jnp.bfloat16)
    grad_send = into_slots(cotangent[source_row])
    grad_recv = lax.all_to_all(grad_send, "exp", split_axis=0, concat_axis=0, tiled=True)
    back_proj = lax.dot_general(
        grad_recv.reshape(-1, model_width),
        w_down[0],
        (((1,), (1,)), ((), ())),
        preferred_element_type=jnp.float32,
    )
    weight_rows = weight_recv.reshape(-1).astype(jnp.float32)
    local_grad = jnp.sum(weight_rows[:, None] * activated * back_proj, axis=0)
    summed = lax.psum(local_grad, "rep")
    return (mixed, summed[None, :])


def solution(mesh):
    in_specs = (
        P(("rep", "exp"), None),
        P(("rep", "exp"), None),
        P(("rep", "exp"), None),
        P(("rep", "exp"), None),
        P("exp", None, None),
        P("exp", None, None),
        P("exp", None, None),
        P("exp", None),
    )
    out_specs = (P(("rep", "exp"), None), P("exp", None))
    return jax.shard_map(shards, mesh=mesh, in_specs=in_specs, out_specs=out_specs, check_vma=False)
```

profile of v0, /device:TPU:92, one launch (start us, length us, event | category | flops | bytes accessed | tf_op | source)
XLA Modules:
  0.0 740.3 jit_solution(17242156580749610135)
XLA Ops:
  1.8 18.0 %reduce-window.6 = s32[64,8,128]{2,1,0:T(8,128)S(1)} reduce-window(s32[64,8,128]{2,1,0:T(8,128)S(1)} %fusion.26, s32[]{:T(128)} %constant.28.clone.1), window={size=1x1x128 pad=0_0x0_0x127_0}, to_apply=%region_0.0 | reduce-window | flops 8323072 | bytes 524292 | tf_op jit(solution)/shard_map/reduce-window
  23.5 7.6 %scatter_custom_fusion.1 = bf16[1152]{0:T(1024)(128)(2,1)S(1)} fusion(s32[1024]{0:T(1024)S(1)} %broadcast_select_fusion, bf16[1024]{0:T(1024)(128)(2,1)S(1)} %reshape.184, bf16[]{:T(256)} %constant.27.clone.1), kind=kCustom, calls=%fused_computation.47 | custom fusion | bytes 2306
  31.9 10.8 %all-to-all-start.2 = ((bf16[64,1,18]{2,1,0:T(2,128)(2,1)}), bf16[64,1,18]{2,1,0:T(2,128)(2,1)S(1)}, u32[]{:S(2)}, u32[]{:S(2)}) async-start(bf16[64,1,18]{2,1,0:T(2,128)(2,1)} %copy.36), calls=%async_computation.2 | async-start | bytes 65536 | tf_op jit(solution)/shard_map/all_to_all | solution.py:26
  42.7 7.7 %gather_fusion = bf16[1024,4096]{1,0:T(8,128)(2,1)} fusion(bf16[128,4096]{1,0:T(8,128)(2,1)S(1)} %copy-done, s32[1024]{0:T(1024)S(1)} %broadcast_clamp_fusion), kind=kCustom, calls=%fused_computation | custom fusion | bytes 16781312 | tf_op jit(solution)/shard_map/gather | solution.py:22
  50.5 18.5 %scatter_custom_fusion = bf16[1152,4096]{1,0:T(8,128)(2,1)} fusion(s32[1024]{0:T(1024)S(1)} %broadcast_select_fusion, bf16[1024,4096]{1,0:T(8,128)(2,1)} %gather_fusion, bf16[]{:T(256)} %constant.27.clone.1), kind=kCustom, calls=%fused_computation.18 | custom fusion | bytes 9437696
  69.0 13.6 %copy.33 = bf16[64,18,4096]{2,1,0:T(8,128)(2,1)} copy(bf16[64,18,4096]{2,0,1:T(8,128)(2,1)} %bitcast.60) | data formatting | bytes 18874368 | tf_op jit(solution)/shard_map/scatter | solution.py:20
  82.7 10.6 %all-to-all-start = ((bf16[64,18,4096]{2,1,0:T(8,128)(2,1)}), bf16[64,18,4096]{2,1,0:T(8,128)(2,1)}, u32[]{:S(2)}, u32[]{:S(2)}) async-start(bf16[64,18,4096]{2,1,0:T(8,128)(2,1)} %copy.33), calls=%async_computation | async-start | bytes 25165824 | tf_op jit(solution)/shard_map/all_to_all | solution.py:25
  93.3 7.8 %gather_fusion.2 = bf16[1024,4096]{1,0:T(8,128)(2,1)} fusion(bf16[128,4096]{1,0:T(8,128)(2,1)S(1)} %copy-done.2, s32[1024]{0:T(1024)S(1)} %broadcast_clamp_fusion), kind=kCustom, calls=%fused_computation.2 | custom fusion | bytes 16781312 | tf_op jit(solution)/shard_map/gather | solution.py:45
  101.1 18.2 %scatter_custom_fusion.2 = bf16[1152,4096]{1,0:T(8,128)(2,1)} fusion(s32[1024]{0:T(1024)S(1)} %broadcast_select_fusion, bf16[1024,4096]{1,0:T(8,128)(2,1)} %gather_fusion.2, bf16[]{:T(256)} %constant.27.clone.1), kind=kCustom, calls=%fused_computation.16 | custom fusion | bytes 9437696
  119.3 13.6 %copy.37 = bf16[64,18,4096]{2,1,0:T(8,128)(2,1)} copy(bf16[64,18,4096]{2,0,1:T(8,128)(2,1)} %bitcast.59) | data formatting | bytes 18874368 | tf_op jit(solution)/shard_map/scatter | solution.py:20
  132.9 159.0 %all-to-all-done = bf16[64,18,4096]{2,1,0:T(8,128)(2,1)} async-done(((bf16[64,18,4096]{2,1,0:T(8,128)(2,1)}), bf16[64,18,4096]{2,1,0:T(8,128)(2,1)}, u32[]{:S(2)}, u32[]{:S(2)}) %all-to-all-start) | async-done | bytes 9437216 | tf_op jit(solution)/shard_map/all_to_all | solution.py:25
  291.9 10.7 %all-to-all-start.3 = ((bf16[64,18,4096]{2,1,0:T(8,128)(2,1)}), bf16[64,18,4096]{2,1,0:T(8,128)(2,1)}, u32[]{:S(2)}, u32[]{:S(2)}) async-start(bf16[64,18,4096]{2,1,0:T(8,128)(2,1)} %copy.37), calls=%async_computation.3 | async-start | bytes 25165824 | tf_op jit(solution)/shard_map/all_to_all | solution.py:46
  302.6 14.2 %reshape.136 = bf16[1152,4096]{1,0:T(8,128)(2,1)} reshape(bf16[64,18,4096]{2,1,0:T(8,128)(2,1)} %all-to-all-done) | data formatting | bytes 18874368 | tf_op jit(solution)/shard_map/reshape | solution.py:28
  316.8 12.0 %fusion.7 = f32[1152,768]{1,0:T(8,128)S(1)} fusion(bf16[1152,4096]{1,0:T(8,128)(2,1)} %reshape.136, bf16[1,4096,768]{2,1,0:T(8,128)(2,1)} %param.12), kind=kOutput, calls=%fused_computation.14 | convolution fusion | flops 7247757312 | bytes 19267584 | tf_op jit(solution)/shard_map/dot_general | solution.py:29
  328.8 13.0 %fusion.13 = f32[1152,768]{1,0:T(8,128)S(1)} fusion(bf16[1152,4096]{1,0:T(8,128)(2,1)S(1)} %copy-done.4, bf16[1,4096,768]{2,1,0:T(8,128)(2,1)} %param.13, f32[1152,768]{1,0:T(8,128)S(1)} %fusion.7), kind=kOutput, calls=%fused_computation.20 | convolution fusion | flops 7252180992 | bytes 22806528 | tf_op jit(solution)/shard_map/dot_general | solution.py:30
  343.6 9.7 %convolution_convert_fusion = bf16[1152,4096]{1,0:T(8,128)(2,1)} fusion(bf16[1,768,4096]{2,1,0:T(8,128)(2,1)S(1)} %bitcast.69, f32[1152,768]{1,0:T(8,128)S(1)} %fusion.13, f32[768]{0:T(1024)S(1)} %reduce.6), kind=kOutput, calls=%fused_computation.6 | convolution fusion | flops 7254245376 | bytes 19270656 | tf_op jit(solution)/shard_map/dot_general | solution.py:33
  353.3 13.9 %reshape.137 = bf16[64,18,4096]{2,1,0:T(8,128)(2,1)} reshape(bf16[1152,4096]{1,0:T(8,128)(2,1)} %convolution_convert_fusion) | data formatting | bytes 18874368 | tf_op jit(solution)/shard_map/reshape | solution.py:35
  367.2 120.2 %all-to-all-done.3 = bf16[64,18,4096]{2,1,0:T(8,128)(2,1)} async-done(((bf16[64,18,4096]{2,1,0:T(8,128)(2,1)}), bf16[64,18,4096]{2,1,0:T(8,128)(2,1)}, u32[]{:S(2)}, u32[]{:S(2)}) %all-to-all-start.3) | async-done | bytes 9437216 | tf_op jit(solution)/shard_map/all_to_all | solution.py:46
  487.5 10.3 %all-to-all-start.1 = ((bf16[64,18,4096]{2,1,0:T(8,128)(2,1)}), bf16[64,18,4096]{2,1,0:T(8,128)(2,1)}, u32[]{:S(2)}, u32[]{:S(2)}) async-start(bf16[64,18,4096]{2,1,0:T(8,128)(2,1)} %reshape.137), calls=%async_computation.1 | async-start | bytes 25165824 | tf_op jit(solution)/shard_map/all_to_all | solution.py:34
  498.2 14.2 %reshape.140 = bf16[1152,4096]{1,0:T(8,128)(2,1)} reshape(bf16[64,18,4096]{2,1,0:T(8,128)(2,1)} %all-to-all-done.3) | data formatting | bytes 18874368 | tf_op jit(solution)/shard_map/reshape | solution.py:48
  512.3 12.5 %fusion.20 = f32[768]{0:T(1024)S(1)} fusion(bf16[1152,4096]{1,0:T(8,128)(2,1)} %reshape.140, bf16[1,768,4096]{2,1,0:T(8,128)(2,1)} %param.14, f32[1152,768]{1,0:T(8,128)} %copy-done.7, f32[1152]{0:T(1024)S(1)} %reshape.153), kind=kOutput, calls=%fused_computation.25 | convolution fusion | flops 7250410496 | bytes 19275264 | tf_op jit(solution)/shard_map/dot_general | solution.py:47
  528.1 157.1 %all-to-all-done.1 = bf16[64,18,4096]{2,1,0:T(8,128)(2,1)} async-done(((bf16[64,18,4096]{2,1,0:T(8,128)(2,1)}), bf16[64,18,4096]{2,1,0:T(8,128)(2,1)}, u32[]{:S(2)}, u32[]{:S(2)}) %all-to-all-start.1) | async-done | bytes 9437216 | tf_op jit(solution)/shard_map/all_to_all | solution.py:34
  685.2 13.4 %copy.34 = bf16[64,18,4096]{2,0,1:T(8,128)(2,1)} copy(bf16[64,18,4096]{2,1,0:T(8,128)(2,1)} %all-to-all-done.1) | data formatting | bytes 18874368 | tf_op jit(solution)/shard_map/all_to_all | solution.py:34
  698.6 33.7 %gather_fusion.1 = bf16[1024,4096]{1,0:T(8,128)(2,1)} fusion(bf16[64,18,4096]{2,0,1:T(8,128)(2,1)} %copy.34, s32[1024]{0:T(1024)S(1)} %bitcast.58), kind=kCustom, calls=%fused_computation.1 | custom fusion | bytes 16785408 | tf_op jit(solution)/shard_map/gather | solution.py:41
  (52 shorter events, 18.8 us)
Async XLA Ops:
  0.6 42.1 %copy-start = (bf16[128,4096]{1,0:T(8,128)(2,1)S(1)}, bf16[128,4096]{1,0:T(8,128)(2,1)}, u32[]{:S(2)}) copy-start(bf16[128,4096]{1,0:T(8,128)(2,1)} %param.8) | copy-start | bytes 3145732
  31.9 50.8 %all-to-all-start.2 = ((bf16[64,1,18]{2,1,0:T(2,128)(2,1)}), bf16[64,1,18]{2,1,0:T(2,128)(2,1)S(1)}, u32[]{:S(2)}, u32[]{:S(2)}) async-start(bf16[64,1,18]{2,1,0:T(2,128)(2,1)} %copy.36), calls=%async_computation.2 | async-start | bytes 65536 | tf_op jit(solution)/shard_map/all_to_all | solution.py:26
  82.7 10.6 %copy-start.2 = (bf16[128,4096]{1,0:T(8,128)(2,1)S(1)}, bf16[128,4096]{1,0:T(8,128)(2,1)}, u32[]{:S(2)}) copy-start(bf16[128,4096]{1,0:T(8,128)(2,1)} %param.11) | copy-start | bytes 3145732
  82.7 209.3 %all-to-all-start = ((bf16[64,18,4096]{2,1,0:T(8,128)(2,1)}), bf16[64,18,4096]{2,1,0:T(8,128)(2,1)}, u32[]{:S(2)}, u32[]{:S(2)}) async-start(bf16[64,18,4096]{2,1,0:T(8,128)(2,1)} %copy.33), calls=%async_computation | async-start | bytes 25165824 | tf_op jit(solution)/shard_map/all_to_all | solution.py:25
  132.9 169.7 %copy-start.6 = (f32[1,768]{1,0:T(1,128)S(1)}, f32[1,768]{1,0:T(1,128)}, u32[]{:S(2)}) copy-start(f32[1,768]{1,0:T(1,128)} %param.15) | copy-start | bytes 9220
  291.9 195.5 %all-to-all-start.3 = ((bf16[64,18,4096]{2,1,0:T(8,128)(2,1)}), bf16[64,18,4096]{2,1,0:T(8,128)(2,1)}, u32[]{:S(2)}, u32[]{:S(2)}) async-start(bf16[64,18,4096]{2,1,0:T(8,128)(2,1)} %copy.37), calls=%async_computation.3 | async-start | bytes 25165824 | tf_op jit(solution)/shard_map/all_to_all | solution.py:46
  316.8 12.0 %copy-start.4 = (bf16[1152,4096]{1,0:T(8,128)(2,1)S(1)}, bf16[1152,4096]{1,0:T(8,128)(2,1)}, u32[]{:S(2)}) copy-start(bf16[1152,4096]{1,0:T(8,128)(2,1)} %reshape.136) | copy-start | bytes 28311556
  316.8 26.8 %slice-start = ((s8[6291456]{0:T(1024)(128)(4,1)}), s8[4194304]{0:T(1024)(128)(4,1)S(1)}, s32[]{:S(2)}) async-start(s8[6291456]{0:T(1024)(128)(4,1)} %bitcast.68), calls=%async_computation.4 | async-start | bytes 8388608
  328.8 14.7 %slice-start.1 = ((s8[6291456]{0:T(1024)(128)(4,1)}), s8[2097152]{0:T(1024)(128)(4,1)S(1)}, s32[]{:S(2)}) async-start(s8[6291456]{0:T(1024)(128)(4,1)} %bitcast.68), calls=%async_computation.5 | async-start | bytes 4194304
  341.8 1.8 copy-start.7
  367.2 130.6 %copy-start.5 = (bf16[128,8]{0,1:T(8,128)(2,1)S(1)}, bf16[128,8]{0,1:T(8,128)(2,1)}, u32[]{:S(2)}) copy-start(bf16[128,8]{0,1:T(8,128)(2,1)} %param.10) | copy-start | bytes 6148
  487.5 197.7 %all-to-all-start.1 = ((bf16[64,18,4096]{2,1,0:T(8,128)(2,1)}), bf16[64,18,4096]{2,1,0:T(8,128)(2,1)}, u32[]{:S(2)}, u32[]{:S(2)}) async-start(bf16[64,18,4096]{2,1,0:T(8,128)(2,1)} %reshape.137), calls=%async_computation.1 | async-start | bytes 25165824 | tf_op jit(solution)/shard_map/all_to_all | solution.py:34
  528.1 170.5 %copy-start.3 = (s32[1024,1]{0,1:T(1,128)S(1)}, s32[1024,1]{0,1:T(1,128)}, u32[]{:S(2)}) copy-start(s32[1024,1]{0,1:T(1,128)} %get-tuple-element.2) | copy-start | bytes 12292
  698.6 41.5 %copy-start.1 = (bf16[128,4096]{1,0:T(8,128)(2,1)S(1)}, bf16[128,4096]{1,0:T(8,128)(2,1)}, u32[]{:S(2)}) copy-start(bf16[128,4096]{1,0:T(8,128)(2,1)} %param.8) | copy-start | bytes 3145732
where the time goes:
time: 747 us; the launch traced here: 740 us
  waiting for transfers between devices  436 us (58%)
  local copies, waits for them, and re-layouts  184 us (25%)
  matrix products  52.8 us (7%)
  starting transfers between devices  42.4 us (6%)
  other arithmetic  20.5 us (3%)
    all_to_all x1, waiting for transfers between devices, shards(): lax.all_to_all(token_send, 'exp', split_axis=0, concat_axis=0, tiled=True)  159 us
    all_to_all x1, waiting for transfers between devices, shards(): lax.all_to_all(expert_out.reshape(owners, capacity, model_width), 'exp',...  157 us
    all_to_all x1, waiting for transfers between devices, shards(): lax.all_to_all(grad_send, 'exp', split_axis=0, concat_axis=0, tiled=True)  120 us
    unnamed x27, local copies, waits for them, and re-layouts  48 us
    gather x1, local copies, waits for them, and re-layouts, shards(): returned[flat_ids, slot_index].reshape(tok_rows, per_token, model_width)  33.7 us
    scatter x2, local copies, waits for them, and re-layouts, into_slots(): return empty.at[flat_ids, slot_index].set(values)  27.3 us
    another operation x3, other arithmetic  18.2 us
  transfers between devices with their start and end apart: 4, of which 3 were waited for; matrix products, arithmetic and copies ran while one was open for 23% of the time, Pallas kernels for 0%

commit v1 on v0

v1 whole, which is shorter than its diff:
```python
import random

import jax
import jax.numpy as jnp
from jax import lax
from jax.experimental import pallas as pl
from jax.experimental.pallas import tpu as pltpu
from jax.sharding import PartitionSpec as P

MESH = pl.DeviceIdType.MESH
BF, F32 = jnp.bfloat16, jnp.float32
TOK, D, FF = 128, 4096, 768
SIDE, PLANE = 4, 16
MAIN, EXTRA, ROWS = 16, 2, 72
WIDE = 1408
OFF = (0, 1408, 2816)
COLS = (1408, 1408, 1280)
STRIDE = (16, 4, 1)
OTHER = ((1, 2), (0, 2), (0, 1))


def plane_order():
    rng = random.Random(1)
    base = [(a, b) for a in range(SIDE) for b in range(SIDE) if a or b]
    rng.shuffle(base)
    order = []
    for a, b in base:
        order += [(0, a, b), (1, b, a), (2, a, b)]
    return order


ORDER = plane_order()


def kernel(tok, cot, cc, wg_hbm, wu_hbm, wd_hbm, scale, mixed, grad, x_hbm, c_hbm, r_hbm,
           t_tok, t_cot, buf_a, buf_b, part, ids, wg, wu, wd, act, hid, stage, ext, pm, acc, gsend, grecv,
           wsem, lsem, ssem, esem, id_s, id_r, bc_s, bc_r, pl_s, pl_r, red_s, red_r, rep_s, rep_r):
    rep = lax.axis_index("rep")
    me = lax.axis_index("exp")
    c = (me // 16, (me // 4) % 4, me % 4)
    sign = 1 - 2 * rep
    own = [c[OTHER[p][0]] * SIDE + c[OTHER[p][1]] for p in range(3)]

    def axis_peer(p, d):
        v = lax.rem(c[p] + d, SIDE)
        return (rep, me + (v - c[p]) * STRIDE[p]), v

    def plane_peer(p, u, w):
        return (rep, c[p] * STRIDE[p] + u * STRIDE[OTHER[p][0]] + w * STRIDE[OTHER[p][1]])

    def near(p, a, b):
        u = lax.rem(c[OTHER[p][0]] + a + SIDE, SIDE)
        w = lax.rem(c[OTHER[p][1]] + b + SIDE, SIDE)
        return u, w

    barrier = pltpu.get_barrier_semaphore()
    greet = {}
    for p in range(3):
        for d in range(1, SIDE):
            off = [0, 0, 0]
            off[p] = d
            greet[tuple(off)] = True
    for p in range(3):
        for a in range(SIDE):
            for b in range(SIDE):
                if a or b:
                    off = [0, 0, 0]
                    off[OTHER[p][0]], off[OTHER[p][1]] = a, b
                    greet[tuple(off)] = True
    for off in greet:
        y, z, x = (lax.rem(c[i] + off[i], SIDE) for i in range(3))
        pl.semaphore_signal(barrier, inc=1, device_id=(rep, y * 16 + z * 4 + x), device_id_type=MESH)
    pl.semaphore_signal(barrier, inc=1, device_id=(1 - rep, me), device_id_type=MESH)

    weights = [pltpu.make_async_copy(s.at[0], t, wsem.at[i])
               for i, (s, t) in enumerate(((wg_hbm, wg), (wu_hbm, wu), (wd_hbm, wd)))]
    mine = []
    for p in range(3):
        cols = pl.ds(0, COLS[p])
        mine.append(pltpu.make_async_copy(cc.at[p, c[p]], ids.at[p, c[p]], lsem.at[p]))
        mine.append(pltpu.make_async_copy(tok.at[:, pl.ds(OFF[p], COLS[p])], t_tok.at[p, c[p], :, cols], lsem.at[3 + p]))
        mine.append(pltpu.make_async_copy(cot.at[:, pl.ds(OFF[p], COLS[p])], t_cot.at[p, c[p], :, cols], lsem.at[6 + p]))
    for copy in mine:
        copy.start()
    pl.semaphore_wait(barrier, len(greet) + 1)

    id_out, bc_out = [], []
    for d in (2, 1, 3):
        for p in range(3):
            peer, v = axis_peer(p, d)
            id_out.append(pltpu.make_async_remote_copy(
                cc.at[p, v], ids.at[p, c[p]], id_s.at[p, d - 1], id_r.at[p, d - 1], device_id=peer, device_id_type=MESH))
    for k, (src, dst) in enumerate(((tok, t_tok), (cot, t_cot))):
        for d in (2, 1, 3):
            for p in range(3):
                peer, _ = axis_peer(p, d)
                bc_out.append(pltpu.make_async_remote_copy(
                    src.at[:, pl.ds(OFF[p], COLS[p])], dst.at[p, c[p], :, pl.ds(0, COLS[p])],
                    bc_s.at[k, p, d - 1], bc_r.at[k, p, d - 1], device_id=peer, device_id_type=MESH))
    for copy in id_out + bc_out:
        copy.start()
    for copy in weights:
        copy.start()

    def id_in(p, d):
        v = lax.rem(c[p] - d + SIDE, SIDE)
        return pltpu.make_async_remote_copy(
            cc.at[p, v], ids.at[p, v], id_s.at[p, d - 1], id_r.at[p, d - 1],
            device_id=axis_peer(p, d)[0], device_id_type=MESH)

    def bc_in(k, p, d):
        v = lax.rem(c[p] - d + SIDE, SIDE)
        src, dst = ((tok, t_tok), (cot, t_cot))[k]
        return pltpu.make_async_remote_copy(
            src.at[:, pl.ds(OFF[p], COLS[p])], dst.at[p, v, :, pl.ds(0, COLS[p])],
            bc_s.at[k, p, d - 1], bc_r.at[k, p, d - 1], device_id=axis_peer(p, d)[0], device_id_type=MESH)

    for p in range(3):
        mine[3 * p].wait()
        for d in range(1, SIDE):
            id_in(p, d).wait_recv()

    row16 = lax.broadcasted_iota(jnp.int32, (MAIN, TOK), 0).astype(F32)
    row8 = lax.broadcasted_iota(jnp.int32, (SIDE * EXTRA, TOK), 0)

    def main_mask(p, v, weigh):
        for uw in range(PLANE):
            code = ids[p, v, 0, uw:uw + 1, :]
            hit = jnp.broadcast_to(code, (MAIN, TOK)) == row16
            value = jnp.broadcast_to(ids[p, v, 1, uw:uw + 1, :], (MAIN, TOK)) if weigh else 1.0
            pm[uw * MAIN:(uw + 1) * MAIN, :] = jnp.where(hit, value, 0.0).astype(BF)

    def extra_mask(p, v, weigh):
        slot = (row8 % EXTRA + MAIN).astype(F32)
        blocks = []
        for uw in range(PLANE):
            code = jnp.broadcast_to(ids[p, v, 0, uw:uw + 1, :], row8.shape)
            value = jnp.broadcast_to(ids[p, v, 1, uw:uw + 1, :], row8.shape) if weigh else 1.0
            blocks.append(jnp.where((code == slot) & (row8 // EXTRA == v), value, 0.0))
        return jnp.concatenate(blocks, axis=0).astype(BF)

    def pick(k, p):
        src = (t_tok, t_cot)[k]
        buf = (buf_a, buf_b)[k]
        n = COLS[p]
        ones = jnp.ones((TOK, 128), BF)
        for d in range(SIDE):
            if d == 0:
                mine[3 * p + 1 + k].wait()
            else:
                bc_in(k, p, d).wait_recv()
            v = lax.rem(c[p] - d + SIDE, SIDE)
            main_mask(p, v, False)
            rows = pl.ds(pl.multiple_of(v * MAIN, MAIN), MAIN)
            got = jnp.dot(pm[...], src[p, v, :, 0:n], preferred_element_type=F32).astype(BF)
            buf[p, :, rows, 0:n] = got.reshape(PLANE, MAIN, n)
            if k == 1 and p == 2:
                main_mask(p, v, True)
                got = jnp.dot(pm[...], ones, preferred_element_type=F32).astype(BF)
                buf[p, :, rows, n:WIDE] = got.reshape(PLANE, MAIN, WIDE - n)
        got = jnp.zeros((PLANE * SIDE * EXTRA, n), F32)
        gotw = jnp.zeros((PLANE * SIDE * EXTRA, WIDE - n), F32) if n < WIDE else None
        for v in range(SIDE):
            got += jnp.dot(extra_mask(p, v, False), src[p, v, :, 0:n], preferred_element_type=F32)
            if k == 1 and p == 2:
                gotw += jnp.dot(extra_mask(p, v, True), ones, preferred_element_type=F32)
        for uw in range(PLANE):
            buf[p, uw, SIDE * MAIN:ROWS, 0:n] = got[uw * 8:uw * 8 + 8].astype(BF)
            if k == 1 and p == 2:
                buf[p, uw, SIDE * MAIN:ROWS, n:WIDE] = gotw[uw * 8:uw * 8 + 8].astype(BF)

    def width(k, p):
        return WIDE if k == 1 else COLS[p]

    LAND = (x_hbm, c_hbm, r_hbm)
    FROM = (buf_a, buf_b, buf_a)

    def hop(k, p, u, w, land):
        n = pl.ds(0, width(k, p))
        there = u * SIDE + w
        at = there if land else own[p]
        return pltpu.make_async_remote_copy(
            FROM[k].at[p, there, :, n], LAND[k].at[p, at, :, n], pl_s.at[k, p, there], pl_r.at[k, p, at],
            device_id=plane_peer(p, u, w), device_id_type=MESH)

    def keep(k, p):
        n = pl.ds(0, width(k, p))
        return pltpu.make_async_copy(FROM[k].at[p, own[p], :, n], LAND[k].at[p, own[p], :, n], ssem.at[k, p])

    def around(p, action):
        def step(i, carry):
            u, w = near(p, i // SIDE, i % SIDE)
            action(u, w)
            return carry
        lax.fori_loop(1, PLANE, step, 0)

    for k in range(2):
        for p in range(3):
            pick(k, p)
        for p, a, b in ORDER:
            u, w = near(p, sign * a, sign * b)
            hop(k, p, u, w, False).start()
        for p in range(3):
            keep(k, p).start()

    def arrived(k, p):
        keep(k, p).wait()
        around(p, lambda u, w: hop(k, p, u, w, True).wait_recv())

    def sent(k, p):
        around(p, lambda u, w: hop(k, p, u, w, False).wait_send())

    def stage_group(k, g, slot):
        src = LAND[k]
        for q in range(PLANE):
            z, x = q // SIDE, q % SIDE
            rows = pl.ds(q * MAIN, MAIN)
            pltpu.make_async_copy(
                src.at[0, q, pl.ds(pl.multiple_of(g * MAIN, MAIN), MAIN), :],
                stage.at[slot, rows, pl.ds(OFF[0], WIDE)], esem.at[slot]).start()
            pltpu.make_async_copy(
                src.at[1, g * SIDE + x, pl.ds(z * MAIN, MAIN), :],
                stage.at[slot, rows, pl.ds(OFF[1], WIDE)], esem.at[slot]).start()
            n = width(k, 2)
            pltpu.make_async_copy(
                src.at[2, g * SIDE + z, pl.ds(x * MAIN, MAIN), pl.ds(0, n)],
                stage.at[slot, rows, pl.ds(OFF[2], n)], esem.at[slot]).start()

    def stage_wait(k, slot):
        n = pl.ds(0, OFF[2] + width(k, 2))
        pltpu.make_async_copy(stage.at[slot, :, n], stage.at[slot, :, n], esem.at[slot]).wait()

    def stage_extra(k):
        src = LAND[k]
        for p in range(3):
            for q in range(PLANE):
                pltpu.make_async_copy(
                    src.at[p, q, pl.ds(SIDE * MAIN, 8), pl.ds(0, width(k, p))],
                    ext.at[pl.ds(q * 8, 8), pl.ds(OFF[p], width(k, p))], esem.at[2]).start()
        n = pl.ds(0, OFF[2] + width(k, 2))
        pltpu.make_async_copy(ext.at[:, n], ext.at[:, n], esem.at[2]).wait()

    ra = lax.broadcasted_iota(jnp.int32, (128, 128), 0)
    rb = lax.broadcasted_iota(jnp.int32, (128, 128), 1)

    def plan_row(p, r):
        pos = (r // 32, (r // 8) % 4, (r // 2) % 4)
        return (pos[OTHER[p][0]] * 4 + pos[OTHER[p][1]]) * 8 + pos[p] * 2 + r % 2

    def to_canon(p):
        return (plan_row(p, ra) == rb).astype(F32).astype(BF)

    def from_canon(p):
        return (plan_row(p, rb) == ra).astype(F32).astype(BF)

    def extra_into_stage(k, slot):
        stage_extra(k)
        for p in range(3):
            cols = slice(OFF[p], OFF[p] + width(k, p))
            block = ext[:, cols]
            if p < 2:
                block = jnp.dot(to_canon(p), block, preferred_element_type=F32).astype(BF)
            stage[slot, 0:128, cols] = block

    def expert(slot, m, row0):
        def tile(i, carry):
            cols = pl.ds(pl.multiple_of(i * 256, 256), 256)
            gate = jnp.dot(stage[slot, 0:m, 0:D], wg[:, cols], preferred_element_type=F32)
            up = jnp.dot(stage[slot, 0:m, 0:D], wu[:, cols], preferred_element_type=F32)
            value = gate / (1.0 + jnp.exp(-gate)) * up
            act[pl.ds(row0, m), cols] = value
            hid[0:m, cols] = (scale[0:1, cols] * value).astype(BF)
            return carry
        lax.fori_loop(0, FF // 256, tile, 0)

    def down(m, p):
        return jnp.dot(hid[0:m, :], wd[:, OFF[p]:OFF[p] + COLS[p]], preferred_element_type=F32).astype(BF)

    for p in range(3):
        arrived(0, p)
    for p in range(3):
        sent(0, p)
    for copy in weights:
        copy.wait()
    stage_group(0, c[0], 0)
    extra_into_stage(0, 1)
    expert(1, 128, 1024)
    for p in range(3):
        out = down(128, p)
        if p < 2:
            out = jnp.dot(from_canon(p), out, preferred_element_type=F32).astype(BF)
        for q in range(PLANE):
            buf_a[p, q, SIDE * MAIN:ROWS, 0:COLS[p]] = out[q * 8:q * 8 + 8]

    def token_group(i, carry):
        slot = i % 2
        g = lax.rem(c[0] + sign * i + SIDE, SIDE)
        stage_wait(0, slot)

        @pl.when(i < SIDE - 1)
        def _():
            stage_group(0, lax.rem(c[0] + sign * (i + 1) + SIDE, SIDE), 1 - slot)

        expert(slot, 256, pl.multiple_of(g * 256, 256))
        out = down(256, 2)
        buf_a[2, pl.ds(g * SIDE, SIDE), 0:SIDE * MAIN, 0:COLS[2]] = out.reshape(SIDE, SIDE * MAIN, COLS[2])
        out = down(256, 1)
        for z in range(SIDE):
            for x in range(SIDE):
                r = (z * SIDE + x) * MAIN
                buf_a[1, g * SIDE + x, z * MAIN:(z + 1) * MAIN, :] = out[r:r + MAIN]
        for w in range(SIDE):
            for p in (1, 2):
                w2 = lax.rem(c[OTHER[p][1]] + w, SIDE)
                if w == 0:
                    @pl.when(i > 0)
                    def _():
                        hop(2, p, g, w2, False).start()
                else:
                    hop(2, p, g, w2, False).start()
        out = down(256, 0)
        buf_a[0, :, pl.ds(pl.multiple_of(g * MAIN, MAIN), MAIN), :] = out.reshape(PLANE, MAIN, COLS[0])
        return carry

    lax.fori_loop(0, SIDE, token_group, 0)
    for p, a, b in ORDER:
        if p == 0:
            u, w = near(p, sign * a, sign * b)
            hop(2, p, u, w, False).start()
    for p in range(3):
        keep(2, p).start()

    for p in range(3):
        arrived(1, p)

    def gradient(slot, m, row0):
        def tile(i, carry):
            cols = pl.ds(pl.multiple_of(i * 256, 256), 256)
            back = lax.dot_general(stage[slot, 0:m, 0:D], wd[cols, :], (((1,), (1,)), ((), ())),
                                   preferred_element_type=F32)
            weight = stage[slot, 0:m, D:D + 128].astype(F32)[:, 0:1]
            acc[0:1, cols] += jnp.sum(weight * act[pl.ds(row0, m), cols] * back, axis=0, keepdims=True)
            return carry
        lax.fori_loop(0, FF // 256, tile, 0)

    acc[...] = jnp.zeros_like(acc)
    stage_group(1, c[0], 0)
    extra_into_stage(1, 1)
    gradient(1, 128, 1024)

    def cot_group(i, carry):
        slot = i % 2
        g = lax.rem(c[0] + sign * i + SIDE, SIDE)
        stage_wait(1, slot)

        @pl.when(i < SIDE - 1)
        def _():
            stage_group(1, lax.rem(c[0] + sign * (i + 1) + SIDE, SIDE), 1 - slot)

        gradient(slot, 256, pl.multiple_of(g * 256, 256))
        return carry

    lax.fori_loop(0, SIDE, cot_group, 0)
    gsend[...] = acc[...]
    pair = pltpu.make_async_remote_copy(gsend, grecv, rep_s, rep_r, device_id=(1 - rep, me), device_id_type=MESH)
    pair.start()

    for p in range(3):
        sent(1, p)
    red_out = []
    for p in (2, 1, 0):
        n = COLS[p]
        arrived(2, p)
        whole = pltpu.make_async_copy(r_hbm.at[p, :, :, pl.ds(0, n)], buf_b.at[p, :, :, pl.ds(0, n)], ssem.at[1, p])
        whole.start()
        for q in range(PLANE):
            pltpu.make_async_copy(
                r_hbm.at[p, q, pl.ds(SIDE * MAIN, 8), pl.ds(0, n)],
                ext.at[pl.ds(q * 8, 8), pl.ds(OFF[p], n)], esem.at[2]).start()
        e = ext.at[:, pl.ds(OFF[p], n)]
        pltpu.make_async_copy(e, e, esem.at[2]).wait()
        whole.wait()
        for d in (1, 2, 3, 0):
            peer, v = axis_peer(p, d)
            main_mask(p, v, True)
            rows = buf_b[p, :, pl.ds(pl.multiple_of(v * MAIN, MAIN), MAIN), 0:n].reshape(PLANE * MAIN, n)
            total = lax.dot_general(pm[...], rows, (((0,), (0,)), ((), ())), preferred_element_type=F32)
            total += lax.dot_general(extra_mask(p, v, True), ext[:, OFF[p]:OFF[p] + n], (((0,), (0,)), ((), ())),
                                     preferred_element_type=F32)
            if d == 0:
                part[p, 0, :, 0:n] = total.astype(BF)
            else:
                t_tok[p, d, :, 0:n] = total.astype(BF)
                copy = pltpu.make_async_remote_copy(
                    t_tok.at[p, d, :, pl.ds(0, n)], part.at[p, d, :, pl.ds(0, n)], red_s.at[p, d - 1], red_r.at[p, d - 1],
                    device_id=peer, device_id_type=MESH)
                copy.start()
                red_out.append((p, copy))
    pair.wait()
    grad[...] = acc[0:1, :] + grecv[0:1, :]
    for p in (2, 1, 0):
        n = COLS[p]
        for q, copy in red_out:
            if q == p:
                copy.wait_recv()
        total = part[p, 0, :, 0:n].astype(F32)
        for d in range(1, SIDE):
            total += part[p, d, :, 0:n].astype(F32)
        mixed[:, OFF[p]:OFF[p] + n] = total.astype(BF)

    for p in range(3):
        sent(2, p)
    for copy in id_out + bc_out:
        copy.wait_send()
    for _, copy in red_out:
        copy.wait_send()


def shards(tokens, expert_ids, route_weights, cotangent, w_gate, w_up, w_down, ia3_scale):
    owners = 64
    ids_t = expert_ids.T
    weights_t = route_weights.T.astype(F32)
    hit = ids_t[:, None, :] == jnp.arange(owners, dtype=jnp.int32)[None, :, None]
    chosen = jnp.sum(hit.astype(F32), axis=0)
    weight = jnp.sum(jnp.where(hit, weights_t[:, None, :], 0.0), axis=0)
    earlier = jnp.arange(TOK)[:, None] < jnp.arange(TOK)[None, :]
    rank = jnp.dot(chosen.astype(BF), earlier.astype(BF), preferred_element_type=F32)
    code = jnp.where(chosen > 0, rank, 99.0)
    both = jnp.stack([code, weight]).reshape(2, 4, 4, 4, TOK)
    cc = jnp.stack([
        both.transpose(1, 0, 2, 3, 4).reshape(4, 2, 16, TOK),
        both.transpose(2, 0, 1, 3, 4).reshape(4, 2, 16, TOK),
        both.transpose(3, 0, 1, 2, 4).reshape(4, 2, 16, TOK),
    ])
    hbm = pl.BlockSpec(memory_space=pl.ANY)
    vmem = pl.BlockSpec(memory_space=pltpu.VMEM)
    land = jax.ShapeDtypeStruct((3, PLANE, ROWS, WIDE), BF)
    dma = pltpu.SemaphoreType.DMA
    out = pl.pallas_call(
        kernel,
        out_shape=[jax.ShapeDtypeStruct((TOK, D), BF), jax.ShapeDtypeStruct((1, FF), F32), land, land, land],
        in_specs=[hbm] * 6 + [vmem],
        out_specs=[vmem, vmem, hbm, hbm, hbm],
        scratch_shapes=[
            pltpu.VMEM((3, SIDE, TOK, WIDE), BF),
            pltpu.VMEM((3, SIDE, TOK, WIDE), BF),
            pltpu.VMEM((3, PLANE, ROWS, WIDE), BF),
            pltpu.VMEM((3, PLANE, ROWS, WIDE), BF),
            pltpu.VMEM((3, SIDE, TOK, WIDE), BF),
            pltpu.VMEM((3, SIDE, 2, PLANE, TOK), F32),
            pltpu.VMEM((D, FF), BF),
            pltpu.VMEM((D, FF), BF),
            pltpu.VMEM((FF, D), BF),
            pltpu.VMEM((1152, FF), F32),
            pltpu.VMEM((256, FF), BF),
            pltpu.VMEM((2, 256, D + 128), BF),
            pltpu.VMEM((128, D + 128), BF),
            pltpu.VMEM((256, TOK), BF),
            pltpu.VMEM((8, FF), F32),
            pltpu.VMEM((8, FF), F32),
            pltpu.VMEM((8, FF), F32),
            dma((3,)), dma((9,)), dma((3, 3)), dma((3,)),
            dma((3, 3)), dma((3, 3)), dma((2, 3, 3)), dma((2, 3, 3)),
            dma((3, 3, PLANE)), dma((3, 3, PLANE)), dma((3, 3)), dma((3, 3)), dma(()), dma(()),
        ],
        compiler_params=pltpu.CompilerParams(collective_id=0, has_side_effects=True, vmem_limit_bytes=67043328),
    )(tokens, cotangent, cc, w_gate, w_up, w_down, ia3_scale)
    return out[0], out[1]


def solution(mesh):
    rows = P(("rep", "exp"), None)
    weights = P("exp", None, None)
    return jax.shard_map(
        shards, mesh=mesh, in_specs=(rows, rows, rows, rows, weights, weights, weights, P("exp", None)),
        out_specs=(rows, P("exp", None)), check_vma=False)
```

time: 747 us -> 318 us (0.43)
  the two profiles are of different devices: /device:TPU:92 before, /device:TPU:0 now
where the time goes in v1:
time: 318 us; the launch traced here: 313 us
  Pallas kernels  306 us (96%)
  local copies, waits for them, and re-layouts  3.57 us (1%)
    pallas_call x1, Pallas kernels, shards(): pl.pallas_call(kernel, out_shape=[jax.ShapeDtypeStruct((TOK, D), BF), jax...  306 us

profile of v1, /device:TPU:0, one launch (start us, length us, event | category | flops | bytes accessed | tf_op | source)
XLA Modules:
  0.0 313.0 jit_solution(2707691004652430326)
XLA Ops:
  0.6 0.7 convert_bitcast_fusion
  1.3 0.7 convert_reduce_fusion
  2.1 0.1 convolution_select_fusion
  2.3 0.7 pad_maximum_fusion.cc
  3.0 306.5 %shard_map.95 = (bf16[128,4096]{1,0:T(8,128)(2,1)}, f32[1,768]{1,0:T(1,128)}, bf16[3,16,72,1408]{3,2,1,0:T(8,128)(2,1)}, bf16[3,16,72,1408]{3,2,1,0:T(8,128)(2,1)}, bf16[3,16,72,1408]{3,2,1,0:T(8,128)(2,1)}) custom-call(bf16[128,4096]{1,0:T(8,128)(2,1)} %tok.1, bf16[128,4096]{1,0:T(8,128)(2,1)} %cot.1, f32[3,4,2,16,128]{4,3,2,1,0:T(8,128)} %pad_maximum_fusion.cc, ...), custom_call_target="tpu_custom_call" | custom-call | tf_op jit(solution)/shard_map/pallas_call | solution.py:439
  309.5 2.3 copy.21
  311.8 1.2 copy.22
  (4 shorter events, 0.1 us)

commit v2 on v1

--- a/solution.py
+++ b/solution.py
@@ -1,5 +1,3 @@
-import random
-
 import jax
 import jax.numpy as jnp
 from jax import lax
@@ -16,29 +14,15 @@
 OFF = (0, 1408, 2816)
 COLS = (1408, 1408, 1280)
 STRIDE = (16, 4, 1)
-OTHER = ((1, 2), (0, 2), (0, 1))
-
-
-def plane_order():
-    rng = random.Random(1)
-    base = [(a, b) for a in range(SIDE) for b in range(SIDE) if a or b]
-    rng.shuffle(base)
-    order = []
-    for a, b in base:
-        order += [(0, a, b), (1, b, a), (2, a, b)]
-    return order
-
-
-ORDER = plane_order()
-
-
-def kernel(tok, cot, cc, wg_hbm, wu_hbm, wd_hbm, scale, mixed, grad, x_hbm, c_hbm, r_hbm,
+OTHER = ((1, 2), (2, 0), (0, 1))
+
+
+def kernel(tok, cot, cc, wg_hbm, wu_hbm, wd_hbm, scale, mixed, grad, x_hbm, c_hbm, r_hbm, y_hbm,
            t_tok, t_cot, buf_a, buf_b, part, ids, wg, wu, wd, act, hid, stage, ext, pm, acc, gsend, grecv,
-           wsem, lsem, ssem, esem, id_s, id_r, bc_s, bc_r, pl_s, pl_r, red_s, red_r, rep_s, rep_r):
+           wsem, lsem, ssem, esem, id_s, id_r, bc_s, bc_r, pl_s, pl_r, y_s, y_r, red_s, red_r, rep_s, rep_r):
     rep = lax.axis_index("rep")
     me = lax.axis_index("exp")
     c = (me // 16, (me // 4) % 4, me % 4)
-    sign = 1 - 2 * rep
     own = [c[OTHER[p][0]] * SIDE + c[OTHER[p][1]] for p in range(3)]
 
     def axis_peer(p, d):
@@ -49,24 +33,10 @@
         return (rep, c[p] * STRIDE[p] + u * STRIDE[OTHER[p][0]] + w * STRIDE[OTHER[p][1]])
 
     def near(p, a, b):
-        u = lax.rem(c[OTHER[p][0]] + a + SIDE, SIDE)
-        w = lax.rem(c[OTHER[p][1]] + b + SIDE, SIDE)
-        return u, w
+        return lax.rem(c[OTHER[p][0]] + a + SIDE, SIDE), lax.rem(c[OTHER[p][1]] + b + SIDE, SIDE)
 
     barrier = pltpu.get_barrier_semaphore()
-    greet = {}
-    for p in range(3):
-        for d in range(1, SIDE):
-            off = [0, 0, 0]
-            off[p] = d
-            greet[tuple(off)] = True
-    for p in range(3):
-        for a in range(SIDE):
-            for b in range(SIDE):
-                if a or b:
-                    off = [0, 0, 0]
-                    off[OTHER[p][0]], off[OTHER[p][1]] = a, b
-                    greet[tuple(off)] = True
+    greet = [tuple(d if i == p else 0 for i in range(3)) for p in range(3) for d in range(1, SIDE)]
     for off in greet:
         y, z, x = (lax.rem(c[i] + off[i], SIDE) for i in range(3))
         pl.semaphore_signal(barrier, inc=1, device_id=(rep, y * 16 + z * 4 + x), device_id_type=MESH)
@@ -175,40 +145,96 @@
     LAND = (x_hbm, c_hbm, r_hbm)
     FROM = (buf_a, buf_b, buf_a)
 
-    def hop(k, p, u, w, land):
+    def hop(k, p, a, b, first):
         n = pl.ds(0, width(k, p))
-        there = u * SIDE + w
-        at = there if land else own[p]
+        u, w = near(p, a, b)
+        src = FROM[k].at[p, u * SIDE + w, :, n]
+        if first:
+            i = (a - 1) * 3 + b - 1
+            dst, sem, to = y_hbm.at[k, p, i, :, n], y_r.at[k, p, i], plane_peer(p, u, c[OTHER[p][1]])
+        else:
+            dst, sem, to = LAND[k].at[p, own[p], :, n], pl_r.at[k, p, a * SIDE + b], plane_peer(p, u, w)
         return pltpu.make_async_remote_copy(
-            FROM[k].at[p, there, :, n], LAND[k].at[p, at, :, n], pl_s.at[k, p, there], pl_r.at[k, p, at],
-            device_id=plane_peer(p, u, w), device_id_type=MESH)
+            src, dst, pl_s.at[k, p, a * SIDE + b], sem, device_id=to, device_id_type=MESH)
+
+    def relay(k, p, a, b):
+        n = pl.ds(0, width(k, p))
+        i = (a - 1) * 3 + b - 1
+        u, _ = near(p, -a, 0)
+        _, w = near(p, 0, b)
+        block = y_hbm.at[k, p, i, :, n]
+        to = plane_peer(p, c[OTHER[p][0]], w)
+        pltpu.make_async_remote_copy(block, block, y_s.at[k, p, i], y_r.at[k, p, i],
+                                     device_id=to, device_id_type=MESH).wait_recv()
+        relay_copy(k, p, a, b, u, to).start()
+
+    def relay_copy(k, p, a, b, u, to):
+        n = pl.ds(0, width(k, p))
+        i = (a - 1) * 3 + b - 1
+        return pltpu.make_async_remote_copy(
+            y_hbm.at[k, p, i, :, n], LAND[k].at[p, u * SIDE + c[OTHER[p][1]], :, n],
+            y_s.at[k, p, i], pl_r.at[k, p, a * SIDE + b], device_id=to, device_id_type=MESH)
+
+    def relays(k, start, stop):
+        def step(i, carry):
+            for p in range(3):
+                relay(k, p, i // 3 + 1, i % 3 + 1)
+            return carry
+        lax.fori_loop(start, stop, step, 0)
 
     def keep(k, p):
         n = pl.ds(0, width(k, p))
         return pltpu.make_async_copy(FROM[k].at[p, own[p], :, n], LAND[k].at[p, own[p], :, n], ssem.at[k, p])
 
-    def around(p, action):
+    def launch(k):
+        for i in range(9):
+            for p in range(3):
+                hop(k, p, i // 3 + 1, i % 3 + 1, True).start()
+        for a in (2, 1, 3):
+            for p in range(3):
+                hop(k, p, 0, a, False).start()
+                hop(k, p, a, 0, False).start()
+        for p in range(3):
+            keep(k, p).start()
+
+    for p in range(3):
+        pick(0, p)
+    launch(0)
+    for p in range(3):
+        pick(1, p)
+    relays(0, 0, 9)
+    launch(1)
+
+    def arrived(k, p):
+        keep(k, p).wait()
+
         def step(i, carry):
-            u, w = near(p, i // SIDE, i % SIDE)
-            action(u, w)
+            n = pl.ds(0, width(k, p))
+            u, w = near(p, -(i // SIDE), -(i % SIDE))
+            block = LAND[k].at[p, u * SIDE + w, :, n]
+            pltpu.make_async_remote_copy(block, block, pl_s.at[k, p, i], pl_r.at[k, p, i],
+                                         device_id=plane_peer(p, u, w), device_id_type=MESH).wait_recv()
             return carry
         lax.fori_loop(1, PLANE, step, 0)
 
-    for k in range(2):
-        for p in range(3):
-            pick(k, p)
-        for p, a, b in ORDER:
-            u, w = near(p, sign * a, sign * b)
-            hop(k, p, u, w, False).start()
-        for p in range(3):
-            keep(k, p).start()
-
-    def arrived(k, p):
-        keep(k, p).wait()
-        around(p, lambda u, w: hop(k, p, u, w, True).wait_recv())
-
     def sent(k, p):
-        around(p, lambda u, w: hop(k, p, u, w, False).wait_send())
+        def step(i, carry):
+            n = pl.ds(0, width(k, p))
+            u, w = near(p, i // SIDE, i % SIDE)
+            block = FROM[k].at[p, u * SIDE + w, :, n]
+            pltpu.make_async_remote_copy(block, block, pl_s.at[k, p, i], pl_r.at[k, p, i],
+                                         device_id=plane_peer(p, u, w), device_id_type=MESH).wait_send()
+            return carry
+        lax.fori_loop(1, PLANE, step, 0)
+
+    def relayed(k, p):
+        def step(i, carry):
+            a, b = i // 3 + 1, i % 3 + 1
+            u, _ = near(p, -a, 0)
+            _, w = near(p, 0, b)
+            relay_copy(k, p, a, b, u, plane_peer(p, c[OTHER[p][0]], w)).wait_send()
+            return carry
+        lax.fori_loop(0, 9, step, 0)
 
     def stage_group(k, g, slot):
         src = LAND[k]
@@ -219,7 +245,7 @@
                 src.at[0, q, pl.ds(pl.multiple_of(g * MAIN, MAIN), MAIN), :],
                 stage.at[slot, rows, pl.ds(OFF[0], WIDE)], esem.at[slot]).start()
             pltpu.make_async_copy(
-                src.at[1, g * SIDE + x, pl.ds(z * MAIN, MAIN), :],
+                src.at[1, x * SIDE + g, pl.ds(z * MAIN, MAIN), :],
                 stage.at[slot, rows, pl.ds(OFF[1], WIDE)], esem.at[slot]).start()
             n = width(k, 2)
             pltpu.make_async_copy(
@@ -294,12 +320,12 @@
 
     def token_group(i, carry):
         slot = i % 2
-        g = lax.rem(c[0] + sign * i + SIDE, SIDE)
+        g = lax.rem(c[0] + i + SIDE, SIDE)
         stage_wait(0, slot)
 
         @pl.when(i < SIDE - 1)
         def _():
-            stage_group(0, lax.rem(c[0] + sign * (i + 1) + SIDE, SIDE), 1 - slot)
+            stage_group(0, lax.rem(c[0] + i + 1 + SIDE, SIDE), 1 - slot)
 
         expert(slot, 256, pl.multiple_of(g * 256, 256))
         out = down(256, 2)
@@ -308,27 +334,49 @@
         for z in range(SIDE):
             for x in range(SIDE):
                 r = (z * SIDE + x) * MAIN
-                buf_a[1, g * SIDE + x, z * MAIN:(z + 1) * MAIN, :] = out[r:r + MAIN]
-        for w in range(SIDE):
-            for p in (1, 2):
-                w2 = lax.rem(c[OTHER[p][1]] + w, SIDE)
-                if w == 0:
-                    @pl.when(i > 0)
-                    def _():
-                        hop(2, p, g, w2, False).start()
-                else:
-                    hop(2, p, g, w2, False).start()
+                buf_a[1, x * SIDE + g, z * MAIN:(z + 1) * MAIN, :] = out[r:r + MAIN]
+        @pl.when(i == 0)
+        def _():
+            for a in (2, 1, 3):
+                hop(2, 1, a, 0, False).start()
+                hop(2, 2, 0, a, False).start()
+
+        @pl.when(i > 0)
+        def _():
+            for a in (1, 2, 3):
+                hop(2, 1, a, i, True).start()
+                hop(2, 2, i, a, True).start()
+            hop(2, 1, 0, i, False).start()
+            hop(2, 2, i, 0, False).start()
+
         out = down(256, 0)
         buf_a[0, :, pl.ds(pl.multiple_of(g * MAIN, MAIN), MAIN), :] = out.reshape(PLANE, MAIN, COLS[0])
+        relays(1, 2 * i, 2 * i + 2)
         return carry
 
     lax.fori_loop(0, SIDE, token_group, 0)
-    for p, a, b in ORDER:
-        if p == 0:
-            u, w = near(p, sign * a, sign * b)
-            hop(2, p, u, w, False).start()
+    for i in range(9):
+        hop(2, 0, i // 3 + 1, i % 3 + 1, True).start()
+    for a in (2, 1, 3):
+        hop(2, 0, 0, a, False).start()
+        hop(2, 0, a, 0, False).start()
     for p in range(3):
         keep(2, p).start()
+    relays(1, 8, 9)
+
+    def relay_returns(i, carry):
+        for a in (1, 2, 3):
+            relay(2, 1, a, i)
+            relay(2, 2, i, a)
+        return carry
+
+    lax.fori_loop(1, SIDE, relay_returns, 0)
+
+    def relay_last(i, carry):
+        relay(2, 0, i // 3 + 1, i % 3 + 1)
+        return carry
+
+    lax.fori_loop(0, 9, relay_last, 0)
 
     for p in range(3):
         arrived(1, p)
@@ -350,12 +398,12 @@
 
     def cot_group(i, carry):
         slot = i % 2
-        g = lax.rem(c[0] + sign * i + SIDE, SIDE)
+        g = lax.rem(c[0] + i + SIDE, SIDE)
         stage_wait(1, slot)
 
         @pl.when(i < SIDE - 1)
         def _():
-            stage_group(1, lax.rem(c[0] + sign * (i + 1) + SIDE, SIDE), 1 - slot)
+            stage_group(1, lax.rem(c[0] + i + 1 + SIDE, SIDE), 1 - slot)
 
         gradient(slot, 256, pl.multiple_of(g * 256, 256))
         return carry
@@ -410,6 +458,8 @@
 
     for p in range(3):
         sent(2, p)
+        for k in range(3):
+            relayed(k, p)
     for copy in id_out + bc_out:
         copy.wait_send()
     for _, copy in red_out:
@@ -429,7 +479,7 @@
     both = jnp.stack([code, weight]).reshape(2, 4, 4, 4, TOK)
     cc = jnp.stack([
         both.transpose(1, 0, 2, 3, 4).reshape(4, 2, 16, TOK),
-        both.transpose(2, 0, 1, 3, 4).reshape(4, 2, 16, TOK),
+        both.transpose(2, 0, 3, 1, 4).reshape(4, 2, 16, TOK),
         both.transpose(3, 0, 1, 2, 4).reshape(4, 2, 16, TOK),
     ])
     hbm = pl.BlockSpec(memory_space=pl.ANY)
@@ -438,9 +488,10 @@
     dma = pltpu.SemaphoreType.DMA
     out = pl.pallas_call(
         kernel,
-        out_shape=[jax.ShapeDtypeStruct((TOK, D), BF), jax.ShapeDtypeStruct((1, FF), F32), land, land, land],
+        out_shape=[jax.ShapeDtypeStruct((TOK, D), BF), jax.ShapeDtypeStruct((1, FF), F32), land, land, land,
+                   jax.ShapeDtypeStruct((3, 3, 9, ROWS, WIDE), BF)],
         in_specs=[hbm] * 6 + [vmem],
-        out_specs=[vmem, vmem, hbm, hbm, hbm],
+        out_specs=[vmem, vmem, hbm, hbm, hbm, hbm],
         scratch_shapes=[
             pltpu.VMEM((3, SIDE, TOK, WIDE), BF),
             pltpu.VMEM((3, SIDE, TOK, WIDE), BF),
@@ -461,7 +512,7 @@
             pltpu.VMEM((8, FF), F32),
             dma((3,)), dma((9,)), dma((3, 3)), dma((3,)),
             dma((3, 3)), dma((3, 3)), dma((2, 3, 3)), dma((2, 3, 3)),
-            dma((3, 3, PLANE)), dma((3, 3, PLANE)), dma((3, 3)), dma((3, 3)), dma(()), dma(()),
+            dma((3, 3, PLANE)), dma((3, 3, PLANE)), dma((3, 3, 9)), dma((3, 3, 9)), dma((3, 3)), dma((3, 3)), dma(()), dma(()),
         ],
         compiler_params=pltpu.CompilerParams(collective_id=0, has_side_effects=True, vmem_limit_bytes=67043328),
     )(tokens, cotangent, cc, w_gate, w_up, w_down, ia3_scale)

time: 318 us -> 286 us (0.90); the launches traced: 313 us -> 286 us
  Pallas kernels: 306 us -> 279 us
    pallas_call x1, Pallas kernels: 306 us -> 279 us  [shards(): pl.pallas_call(kernel, out_shape=[jax.ShapeDtypeStruct((TOK, D), BF), jax...]
where the time goes in v2:
time: 286 us
  Pallas kernels  279 us (98%)
  local copies, waits for them, and re-layouts  3.6 us (1%)
    pallas_call x1, Pallas kernels, shards(): pl.pallas_call(kernel, out_shape=[jax.ShapeDtypeStruct((TOK, D), BF), jax...  279 us

profile of v2, /device:TPU:0, one launch (start us, length us, event | category | flops | bytes accessed | tf_op | source)
XLA Modules:
  0.0 285.9 jit_solution(6610997001050225789)
XLA Ops:
  0.6 0.7 convert_bitcast_fusion
  1.3 0.7 convert_reduce_fusion
  2.1 0.1 convolution_select_fusion
  2.3 0.7 pad_maximum_fusion.cc
  3.0 279.3 %shard_map.95 = (bf16[128,4096]{1,0:T(8,128)(2,1)}, f32[1,768]{1,0:T(1,128)}, bf16[3,16,72,1408]{3,2,1,0:T(8,128)(2,1)}, bf16[3,16,72,1408]{3,2,1,0:T(8,128)(2,1...) custom-call(bf16[128,4096]{1,0:T(8,128)(2,1)} %tok.1, bf16[128,4096]{1,0:T(8,128)(2,1)} %cot.1, ...), custom_call_target="tpu_custom_call" | custom-call | tf_op jit(solution)/shard_map/pallas_call | solution.py:489
  282.3 2.3 copy.21
  284.6 1.3 copy.22
  (4 shorter events, 0.1 us)

commit v3 on v2

--- a/solution.py
+++ b/solution.py
@@ -17,9 +17,9 @@
 OTHER = ((1, 2), (2, 0), (0, 1))
 
 
-def kernel(tok, cot, cc, wg_hbm, wu_hbm, wd_hbm, scale, mixed, grad, x_hbm, c_hbm, r_hbm, y_hbm,
-           t_tok, t_cot, buf_a, buf_b, part, ids, wg, wu, wd, act, hid, stage, ext, pm, acc, gsend, grecv,
-           wsem, lsem, ssem, esem, id_s, id_r, bc_s, bc_r, pl_s, pl_r, y_s, y_r, red_s, red_r, rep_s, rep_r):
+def kernel(tok, cot, cc, wg_hbm, wu_hbm, wd_hbm, scale, part, grad, x_hbm, c_hbm, r_hbm, y_hbm,
+           t_tok, t_cot, buf_a, buf_b, r_last, ids, wg, wu, wd, act, hid, stage, ext, pm, acc, gsend, grecv,
+           wsem, lsem, ssem, esem, id_s, id_r, bc_s, bc_r, hf_s, hf_r, pl_s, pl_r, y_s, y_r, red_s, red_r, rep_s, rep_r):
     rep = lax.axis_index("rep")
     me = lax.axis_index("exp")
     c = (me // 16, (me // 4) % 4, me % 4)
@@ -54,20 +54,20 @@
         copy.start()
     pl.semaphore_wait(barrier, len(greet) + 1)
 
-    id_out, bc_out = [], []
+    outgoing = []
     for d in (2, 1, 3):
         for p in range(3):
             peer, v = axis_peer(p, d)
-            id_out.append(pltpu.make_async_remote_copy(
+            outgoing.append(pltpu.make_async_remote_copy(
                 cc.at[p, v], ids.at[p, c[p]], id_s.at[p, d - 1], id_r.at[p, d - 1], device_id=peer, device_id_type=MESH))
     for k, (src, dst) in enumerate(((tok, t_tok), (cot, t_cot))):
-        for d in (2, 1, 3):
+        for d in (1, 3):
             for p in range(3):
                 peer, _ = axis_peer(p, d)
-                bc_out.append(pltpu.make_async_remote_copy(
+                outgoing.append(pltpu.make_async_remote_copy(
                     src.at[:, pl.ds(OFF[p], COLS[p])], dst.at[p, c[p], :, pl.ds(0, COLS[p])],
                     bc_s.at[k, p, d - 1], bc_r.at[k, p, d - 1], device_id=peer, device_id_type=MESH))
-    for copy in id_out + bc_out:
+    for copy in outgoing:
         copy.start()
     for copy in weights:
         copy.start()
@@ -79,17 +79,32 @@
             device_id=axis_peer(p, d)[0], device_id_type=MESH)
 
     def bc_in(k, p, d):
-        v = lax.rem(c[p] - d + SIDE, SIDE)
-        src, dst = ((tok, t_tok), (cot, t_cot))[k]
+        block = (t_tok, t_cot)[k].at[p, lax.rem(c[p] - d + SIDE, SIDE), :, pl.ds(0, COLS[p])]
         return pltpu.make_async_remote_copy(
-            src.at[:, pl.ds(OFF[p], COLS[p])], dst.at[p, v, :, pl.ds(0, COLS[p])],
-            bc_s.at[k, p, d - 1], bc_r.at[k, p, d - 1], device_id=axis_peer(p, d)[0], device_id_type=MESH)
+            block, block, bc_s.at[k, p, d - 1], bc_r.at[k, p, d - 1], device_id=axis_peer(p, d)[0], device_id_type=MESH)
+
+    def half(k, p, d, back):
+        v = lax.rem(c[p] - (2 if back else d) + SIDE, SIDE)
+        i = d // 2
+        block = (t_tok, t_cot)[k].at[p, v, pl.ds(i * 64, 64), pl.ds(0, COLS[p])]
+        return pltpu.make_async_remote_copy(
+            block, block, hf_s.at[k, p, i], hf_r.at[k, p, i], device_id=axis_peer(p, d)[0], device_id_type=MESH)
+
+    def forward(k):
+        for d in (1, 3):
+            for p in range(3):
+                bc_in(k, p, d).wait_recv()
+                copy = half(k, p, d, False)
+                copy.start()
+                outgoing.append(copy)
 
     for p in range(3):
         mine[3 * p].wait()
         for d in range(1, SIDE):
             id_in(p, d).wait_recv()
 
+    FROM = (buf_a, buf_b, buf_a)
+    SPREAD = (t_tok, t_cot)
     row16 = lax.broadcasted_iota(jnp.int32, (MAIN, TOK), 0).astype(F32)
     row8 = lax.broadcasted_iota(jnp.int32, (SIDE * EXTRA, TOK), 0)
 
@@ -109,56 +124,43 @@
             blocks.append(jnp.where((code == slot) & (row8 // EXTRA == v), value, 0.0))
         return jnp.concatenate(blocks, axis=0).astype(BF)
 
-    def pick(k, p):
-        src = (t_tok, t_cot)[k]
-        buf = (buf_a, buf_b)[k]
+    def pick(k, p, d):
         n = COLS[p]
-        ones = jnp.ones((TOK, 128), BF)
-        for d in range(SIDE):
-            if d == 0:
-                mine[3 * p + 1 + k].wait()
-            else:
-                bc_in(k, p, d).wait_recv()
-            v = lax.rem(c[p] - d + SIDE, SIDE)
-            main_mask(p, v, False)
-            rows = pl.ds(pl.multiple_of(v * MAIN, MAIN), MAIN)
-            got = jnp.dot(pm[...], src[p, v, :, 0:n], preferred_element_type=F32).astype(BF)
-            buf[p, :, rows, 0:n] = got.reshape(PLANE, MAIN, n)
-            if k == 1 and p == 2:
-                main_mask(p, v, True)
-                got = jnp.dot(pm[...], ones, preferred_element_type=F32).astype(BF)
-                buf[p, :, rows, n:WIDE] = got.reshape(PLANE, MAIN, WIDE - n)
+        v = lax.rem(c[p] - d + SIDE, SIDE)
+        main_mask(p, v, k == 1)
+        rows = pl.ds(pl.multiple_of(v * MAIN, MAIN), MAIN)
+        got = jnp.dot(pm[...], SPREAD[k][p, v, :, 0:n], preferred_element_type=F32).astype(BF)
+        FROM[k][p, :, rows, 0:n] = got.reshape(PLANE, MAIN, n)
+
+    def pick_extra(k, p):
+        n = COLS[p]
         got = jnp.zeros((PLANE * SIDE * EXTRA, n), F32)
-        gotw = jnp.zeros((PLANE * SIDE * EXTRA, WIDE - n), F32) if n < WIDE else None
         for v in range(SIDE):
-            got += jnp.dot(extra_mask(p, v, False), src[p, v, :, 0:n], preferred_element_type=F32)
-            if k == 1 and p == 2:
-                gotw += jnp.dot(extra_mask(p, v, True), ones, preferred_element_type=F32)
+            got += jnp.dot(extra_mask(p, v, k == 1), SPREAD[k][p, v, :, 0:n], preferred_element_type=F32)
         for uw in range(PLANE):
-            buf[p, uw, SIDE * MAIN:ROWS, 0:n] = got[uw * 8:uw * 8 + 8].astype(BF)
-            if k == 1 and p == 2:
-                buf[p, uw, SIDE * MAIN:ROWS, n:WIDE] = gotw[uw * 8:uw * 8 + 8].astype(BF)
-
-    def width(k, p):
-        return WIDE if k == 1 else COLS[p]
-
-    LAND = (x_hbm, c_hbm, r_hbm)
-    FROM = (buf_a, buf_b, buf_a)
+            FROM[k][p, uw, SIDE * MAIN:ROWS, 0:n] = got[uw * 8:uw * 8 + 8].astype(BF)
+
+    def land(k, p, at):
+        n = pl.ds(0, COLS[p])
+        if k == 2 and p == 0:
+            return r_last.at[at, :, n]
+        return (x_hbm, c_hbm, r_hbm)[k].at[p, at, :, n]
+
 
     def hop(k, p, a, b, first):
-        n = pl.ds(0, width(k, p))
+        n = pl.ds(0, COLS[p])
         u, w = near(p, a, b)
         src = FROM[k].at[p, u * SIDE + w, :, n]
         if first:
             i = (a - 1) * 3 + b - 1
             dst, sem, to = y_hbm.at[k, p, i, :, n], y_r.at[k, p, i], plane_peer(p, u, c[OTHER[p][1]])
         else:
-            dst, sem, to = LAND[k].at[p, own[p], :, n], pl_r.at[k, p, a * SIDE + b], plane_peer(p, u, w)
+            dst, sem, to = land(k, p, own[p]), pl_r.at[k, p, a * SIDE + b], plane_peer(p, u, w)
         return pltpu.make_async_remote_copy(
             src, dst, pl_s.at[k, p, a * SIDE + b], sem, device_id=to, device_id_type=MESH)
 
     def relay(k, p, a, b):
-        n = pl.ds(0, width(k, p))
+        n = pl.ds(0, COLS[p])
         i = (a - 1) * 3 + b - 1
         u, _ = near(p, -a, 0)
         _, w = near(p, 0, b)
@@ -169,10 +171,10 @@
         relay_copy(k, p, a, b, u, to).start()
 
     def relay_copy(k, p, a, b, u, to):
-        n = pl.ds(0, width(k, p))
+        n = pl.ds(0, COLS[p])
         i = (a - 1) * 3 + b - 1
         return pltpu.make_async_remote_copy(
-            y_hbm.at[k, p, i, :, n], LAND[k].at[p, u * SIDE + c[OTHER[p][1]], :, n],
+            y_hbm.at[k, p, i, :, n], land(k, p, u * SIDE + c[OTHER[p][1]]),
             y_s.at[k, p, i], pl_r.at[k, p, a * SIDE + b], device_id=to, device_id_type=MESH)
 
     def relays(k, start, stop):
@@ -183,8 +185,8 @@
         lax.fori_loop(start, stop, step, 0)
 
     def keep(k, p):
-        n = pl.ds(0, width(k, p))
-        return pltpu.make_async_copy(FROM[k].at[p, own[p], :, n], LAND[k].at[p, own[p], :, n], ssem.at[k, p])
+        n = pl.ds(0, COLS[p])
+        return pltpu.make_async_copy(FROM[k].at[p, own[p], :, n], land(k, p, own[p]), ssem.at[k, p])
 
     def launch(k):
         for i in range(9):
@@ -197,11 +199,29 @@
         for p in range(3):
             keep(k, p).start()
 
-    for p in range(3):
-        pick(0, p)
+    def far(k, p):
+        for d in (1, 3):
+            half(k, p, d, True).wait_recv()
+
+    forward(0)
+    for p in range(3):
+        mine[3 * p + 1].wait()
+        for d in (0, 1, 3):
+            pick(0, p, d)
+    forward(1)
+    for p in range(3):
+        far(0, p)
+        pick(0, p, 2)
+        pick_extra(0, p)
     launch(0)
     for p in range(3):
-        pick(1, p)
+        mine[3 * p + 2].wait()
+        for d in (0, 1, 3):
+            pick(1, p, d)
+    for p in range(3):
+        far(1, p)
+        pick(1, p, 2)
+        pick_extra(1, p)
     relays(0, 0, 9)
     launch(1)
 
@@ -209,9 +229,8 @@
         keep(k, p).wait()
 
         def step(i, carry):
-            n = pl.ds(0, width(k, p))
             u, w = near(p, -(i // SIDE), -(i % SIDE))
-            block = LAND[k].at[p, u * SIDE + w, :, n]
+            block = land(k, p, u * SIDE + w)
             pltpu.make_async_remote_copy(block, block, pl_s.at[k, p, i], pl_r.at[k, p, i],
                                          device_id=plane_peer(p, u, w), device_id_type=MESH).wait_recv()
             return carry
@@ -219,7 +238,7 @@
 
     def sent(k, p):
         def step(i, carry):
-            n = pl.ds(0, width(k, p))
+            n = pl.ds(0, COLS[p])
             u, w = near(p, i // SIDE, i % SIDE)
             block = FROM[k].at[p, u * SIDE + w, :, n]
             pltpu.make_async_remote_copy(block, block, pl_s.at[k, p, i], pl_r.at[k, p, i],
@@ -237,7 +256,7 @@
         lax.fori_loop(0, 9, step, 0)
 
     def stage_group(k, g, slot):
-        src = LAND[k]
+        src = (x_hbm, c_hbm)[k]
         for q in range(PLANE):
             z, x = q // SIDE, q % SIDE
             rows = pl.ds(q * MAIN, MAIN)
@@ -247,24 +266,22 @@
             pltpu.make_async_copy(
                 src.at[1, x * SIDE + g, pl.ds(z * MAIN, MAIN), :],
                 stage.at[slot, rows, pl.ds(OFF[1], WIDE)], esem.at[slot]).start()
-            n = width(k, 2)
+            n = COLS[2]
             pltpu.make_async_copy(
                 src.at[2, g * SIDE + z, pl.ds(x * MAIN, MAIN), pl.ds(0, n)],
                 stage.at[slot, rows, pl.ds(OFF[2], n)], esem.at[slot]).start()
 
     def stage_wait(k, slot):
-        n = pl.ds(0, OFF[2] + width(k, 2))
-        pltpu.make_async_copy(stage.at[slot, :, n], stage.at[slot, :, n], esem.at[slot]).wait()
+        pltpu.make_async_copy(stage.at[slot], stage.at[slot], esem.at[slot]).wait()
 
     def stage_extra(k):
-        src = LAND[k]
+        src = (x_hbm, c_hbm)[k]
         for p in range(3):
             for q in range(PLANE):
                 pltpu.make_async_copy(
-                    src.at[p, q, pl.ds(SIDE * MAIN, 8), pl.ds(0, width(k, p))],
-                    ext.at[pl.ds(q * 8, 8), pl.ds(OFF[p], width(k, p))], esem.at[2]).start()
-        n = pl.ds(0, OFF[2] + width(k, 2))
-        pltpu.make_async_copy(ext.at[:, n], ext.at[:, n], esem.at[2]).wait()
+                    src.at[p, q, pl.ds(SIDE * MAIN, 8), pl.ds(0, COLS[p])],
+                    ext.at[pl.ds(q * 8, 8), pl.ds(OFF[p], COLS[p])], esem.at[2]).start()
+        pltpu.make_async_copy(ext, ext, esem.at[2]).wait()
 
     ra = lax.broadcasted_iota(jnp.int32, (128, 128), 0)
     rb = lax.broadcasted_iota(jnp.int32, (128, 128), 1)
@@ -282,7 +299,7 @@
     def extra_into_stage(k, slot):
         stage_extra(k)
         for p in range(3):
-            cols = slice(OFF[p], OFF[p] + width(k, p))
+            cols = slice(OFF[p], OFF[p] + COLS[p])
             block = ext[:, cols]
             if p < 2:
                 block = jnp.dot(to_canon(p), block, preferred_element_type=F32).astype(BF)
@@ -386,8 +403,7 @@
             cols = pl.ds(pl.multiple_of(i * 256, 256), 256)
             back = lax.dot_general(stage[slot, 0:m, 0:D], wd[cols, :], (((1,), (1,)), ((), ())),
                                    preferred_element_type=F32)
-            weight = stage[slot, 0:m, D:D + 128].astype(F32)[:, 0:1]
-            acc[0:1, cols] += jnp.sum(weight * act[pl.ds(row0, m), cols] * back, axis=0, keepdims=True)
+            acc[0:1, cols] += jnp.sum(act[pl.ds(row0, m), cols] * back, axis=0, keepdims=True)
             return carry
         lax.fori_loop(0, FF // 256, tile, 0)
 
@@ -415,55 +431,51 @@
 
     for p in range(3):
         sent(1, p)
+    for copy in outgoing:
+        copy.wait_send()
     red_out = []
     for p in (2, 1, 0):
         n = COLS[p]
         arrived(2, p)
-        whole = pltpu.make_async_copy(r_hbm.at[p, :, :, pl.ds(0, n)], buf_b.at[p, :, :, pl.ds(0, n)], ssem.at[1, p])
-        whole.start()
-        for q in range(PLANE):
-            pltpu.make_async_copy(
-                r_hbm.at[p, q, pl.ds(SIDE * MAIN, 8), pl.ds(0, n)],
-                ext.at[pl.ds(q * 8, 8), pl.ds(OFF[p], n)], esem.at[2]).start()
-        e = ext.at[:, pl.ds(OFF[p], n)]
-        pltpu.make_async_copy(e, e, esem.at[2]).wait()
-        whole.wait()
-        for d in (1, 2, 3, 0):
+        if p == 0:
+            block = r_last
+            left = jnp.concatenate([r_last[q, SIDE * MAIN:ROWS, :].astype(F32) for q in range(PLANE)], axis=0)
+            ext[:, OFF[p]:OFF[p] + n] = left.astype(BF)
+        else:
+            block = buf_b.at[p]
+            whole = pltpu.make_async_copy(r_hbm.at[p, :, :, pl.ds(0, n)], buf_b.at[p, :, :, pl.ds(0, n)], ssem.at[1, p])
+            whole.start()
+            for q in range(PLANE):
+                pltpu.make_async_copy(
+                    r_hbm.at[p, q, pl.ds(SIDE * MAIN, 8), pl.ds(0, n)],
+                    ext.at[pl.ds(q * 8, 8), pl.ds(OFF[p], n)], esem.at[2]).start()
+            e = ext.at[:, pl.ds(OFF[p], n)]
+            pltpu.make_async_copy(e, e, esem.at[2]).wait()
+            whole.wait()
+        for d in (2, 1, 3, 0):
             peer, v = axis_peer(p, d)
             main_mask(p, v, True)
-            rows = buf_b[p, :, pl.ds(pl.multiple_of(v * MAIN, MAIN), MAIN), 0:n].reshape(PLANE * MAIN, n)
+            rows = block[:, pl.ds(pl.multiple_of(v * MAIN, MAIN), MAIN), 0:n].reshape(PLANE * MAIN, n)
             total = lax.dot_general(pm[...], rows, (((0,), (0,)), ((), ())), preferred_element_type=F32)
             total += lax.dot_general(extra_mask(p, v, True), ext[:, OFF[p]:OFF[p] + n], (((0,), (0,)), ((), ())),
                                      preferred_element_type=F32)
+            t_tok[p, d, :, 0:n] = total.astype(BF)
+            src, dst = t_tok.at[p, d, :, pl.ds(0, n)], part.at[d, :, pl.ds(OFF[p], n)]
             if d == 0:
-                part[p, 0, :, 0:n] = total.astype(BF)
+                copy = pltpu.make_async_copy(src, dst, lsem.at[p])
             else:
-                t_tok[p, d, :, 0:n] = total.astype(BF)
                 copy = pltpu.make_async_remote_copy(
-                    t_tok.at[p, d, :, pl.ds(0, n)], part.at[p, d, :, pl.ds(0, n)], red_s.at[p, d - 1], red_r.at[p, d - 1],
-                    device_id=peer, device_id_type=MESH)
-                copy.start()
-                red_out.append((p, copy))
+                    src, dst, red_s.at[p, d - 1], red_r.at[p, d - 1], device_id=peer, device_id_type=MESH)
+            copy.start()
+            red_out.append(copy)
     pair.wait()
     grad[...] = acc[0:1, :] + grecv[0:1, :]
-    for p in (2, 1, 0):
-        n = COLS[p]
-        for q, copy in red_out:
-            if q == p:
-                copy.wait_recv()
-        total = part[p, 0, :, 0:n].astype(F32)
-        for d in range(1, SIDE):
-            total += part[p, d, :, 0:n].astype(F32)
-        mixed[:, OFF[p]:OFF[p] + n] = total.astype(BF)
-
     for p in range(3):
         sent(2, p)
         for k in range(3):
             relayed(k, p)
-    for copy in id_out + bc_out:
-        copy.wait_send()
-    for _, copy in red_out:
-        copy.wait_send()
+    for copy in red_out:
+        copy.wait()
 
 
 def shards(tokens, expert_ids, route_weights, cotangent, w_gate, w_up, w_down, ia3_scale):
@@ -488,35 +500,35 @@
     dma = pltpu.SemaphoreType.DMA
     out = pl.pallas_call(
         kernel,
-        out_shape=[jax.ShapeDtypeStruct((TOK, D), BF), jax.ShapeDtypeStruct((1, FF), F32), land, land, land,
+        out_shape=[jax.ShapeDtypeStruct((SIDE, TOK, D), BF), jax.ShapeDtypeStruct((1, FF), F32), land, land, land,
                    jax.ShapeDtypeStruct((3, 3, 9, ROWS, WIDE), BF)],
         in_specs=[hbm] * 6 + [vmem],
-        out_specs=[vmem, vmem, hbm, hbm, hbm, hbm],
+        out_specs=[hbm, vmem, hbm, hbm, hbm, hbm],
         scratch_shapes=[
             pltpu.VMEM((3, SIDE, TOK, WIDE), BF),
             pltpu.VMEM((3, SIDE, TOK, WIDE), BF),
             pltpu.VMEM((3, PLANE, ROWS, WIDE), BF),
             pltpu.VMEM((3, PLANE, ROWS, WIDE), BF),
-            pltpu.VMEM((3, SIDE, TOK, WIDE), BF),
+            pltpu.VMEM((PLANE, ROWS, WIDE), BF),
             pltpu.VMEM((3, SIDE, 2, PLANE, TOK), F32),
             pltpu.VMEM((D, FF), BF),
             pltpu.VMEM((D, FF), BF),
             pltpu.VMEM((FF, D), BF),
             pltpu.VMEM((1152, FF), F32),
             pltpu.VMEM((256, FF), BF),
-            pltpu.VMEM((2, 256, D + 128), BF),
-            pltpu.VMEM((128, D + 128), BF),
+            pltpu.VMEM((2, 256, D), BF),
+            pltpu.VMEM((128, D), BF),
             pltpu.VMEM((256, TOK), BF),
             pltpu.VMEM((8, FF), F32),
             pltpu.VMEM((8, FF), F32),
             pltpu.VMEM((8, FF), F32),
             dma((3,)), dma((9,)), dma((3, 3)), dma((3,)),
-            dma((3, 3)), dma((3, 3)), dma((2, 3, 3)), dma((2, 3, 3)),
+            dma((3, 3)), dma((3, 3)), dma((2, 3, 3)), dma((2, 3, 3)), dma((2, 3, 2)), dma((2, 3, 2)),
             dma((3, 3, PLANE)), dma((3, 3, PLANE)), dma((3, 3, 9)), dma((3, 3, 9)), dma((3, 3)), dma((3, 3)), dma(()), dma(()),
         ],
         compiler_params=pltpu.CompilerParams(collective_id=0, has_side_effects=True, vmem_limit_bytes=67043328),
     )(tokens, cotangent, cc, w_gate, w_up, w_down, ia3_scale)
-    return out[0], out[1]
+    return jnp.sum(out[0].astype(F32), axis=0).astype(BF), out[1]
 
 
 def solution(mesh):

time: 286 us -> 276 us (0.965)
  Pallas kernels: 279 us -> 265 us
  other arithmetic: 2.15 us -> 6.38 us
    pallas_call x1, Pallas kernels: 279 us -> 265 us  [shards(): pl.pallas_call(kernel, out_shape=[jax.ShapeDtypeStruct((SIDE, TOK, D), BF...]
    reduce_sum x0 -> x1, other arithmetic: none -> 4.23 us  [shards(): return (jnp.sum(out[0].astype(F32), axis=0).astype(BF), out[1])]
where the time goes in v3:
time: 276 us; the launch traced here: 274 us
  Pallas kernels  265 us (96%)
  other arithmetic  6.38 us (2%)
    pallas_call x1, Pallas kernels, shards(): pl.pallas_call(kernel, out_shape=[jax.ShapeDtypeStruct((SIDE, TOK, D), BF...  265 us

profile of v3, /device:TPU:0, one launch (start us, length us, event | category | flops | bytes accessed | tf_op | source)
XLA Modules:
  0.0 273.6 jit_solution(17239412073713294637)
XLA Ops:
  0.6 0.7 convert_bitcast_fusion
  1.3 0.7 convert_reduce_fusion
  2.1 0.1 convolution_select_fusion
  2.3 0.7 pad_maximum_fusion.cc
  3.0 265.1 %shard_map.95 = (bf16[4,128,4096]{2,1,0:T(8,128)(2,1)}, f32[1,768]{1,0:T(1,128)}, bf16[3,16,72,1408]{3,2,1,0:T(8,128)(2,1)}, bf16[3,16,72,1408]{3,2,1,0:T(8,128)...) custom-call(bf16[128,4096]{1,0:T(8,128)(2,1)} %tok.1, bf16[128,4096]{1,0:T(8,128)(2,1)} %cot.1, ...), custom_call_target="tpu_custom_call" | custom-call | tf_op jit(solution)/shard_map/pallas_call | solution.py:501
  268.1 4.2 %reduce_sum.32 = bf16[128,4096]{1,0:T(8,128)(2,1)} reduce(bf16[4,128,4096]{2,1,0:T(8,128)(2,1)} %get-tuple-element.4, bf16[]{:T(256)} %constant.6.clone.1), dimensions={0}, to_apply=%region_2.3 | reduce | flops 1572864 | bytes 5242882 | tf_op jit(solution)/shard_map/reduce_sum | solution.py:531
  272.3 1.2 copy.20
  (4 shorter events, 0.1 us)

commit v4 on v3

--- a/solution.py
+++ b/solution.py
@@ -11,15 +11,15 @@
 SIDE, PLANE = 4, 16
 MAIN, EXTRA, ROWS = 16, 2, 72
 WIDE = 1408
-OFF = (0, 1408, 2816)
-COLS = (1408, 1408, 1280)
+COLS = ((1408, 1408, 1280), (1408, 1280, 1408), (1280, 1408, 1408))
+OFF = tuple((0, n[0], n[0] + n[1]) for n in COLS)
 STRIDE = (16, 4, 1)
 OTHER = ((1, 2), (2, 0), (0, 1))
 
 
 def kernel(tok, cot, cc, wg_hbm, wu_hbm, wd_hbm, scale, part, grad, x_hbm, c_hbm, r_hbm, y_hbm,
-           t_tok, t_cot, buf_a, buf_b, r_last, ids, wg, wu, wd, act, hid, stage, ext, pm, acc, gsend, grecv,
-           wsem, lsem, ssem, esem, id_s, id_r, bc_s, bc_r, hf_s, hf_r, pl_s, pl_r, y_s, y_r, red_s, red_r, rep_s, rep_r):
+           t_tok, t_cot, buf_a, buf_b, r_last, ids, wg, wu, wd, act, hid, stage, ext, side, pm, acc, gsend, grecv,
+           wsem, lsem, ssem, esem, id_s, id_r, bc_s, bc_r, hf_s, hf_r, pl_s, pl_r, y_s, y_r, sd_s, sd_r, red_s, red_r, rep_s, rep_r):
     rep = lax.axis_index("rep")
     me = lax.axis_index("exp")
     c = (me // 16, (me // 4) % 4, me % 4)
@@ -46,10 +46,9 @@
                for i, (s, t) in enumerate(((wg_hbm, wg), (wu_hbm, wu), (wd_hbm, wd)))]
     mine = []
     for p in range(3):
-        cols = pl.ds(0, COLS[p])
         mine.append(pltpu.make_async_copy(cc.at[p, c[p]], ids.at[p, c[p]], lsem.at[p]))
-        mine.append(pltpu.make_async_copy(tok.at[:, pl.ds(OFF[p], COLS[p])], t_tok.at[p, c[p], :, cols], lsem.at[3 + p]))
-        mine.append(pltpu.make_async_copy(cot.at[:, pl.ds(OFF[p], COLS[p])], t_cot.at[p, c[p], :, cols], lsem.at[6 + p]))
+        mine.append(pltpu.make_async_copy(tok.at[:, pl.ds(OFF[0][p], COLS[0][p])], t_tok.at[p, c[p], :, pl.ds(0, COLS[0][p])], lsem.at[3 + p]))
+        mine.append(pltpu.make_async_copy(cot.at[:, pl.ds(OFF[1][p], COLS[1][p])], t_cot.at[p, c[p], :, pl.ds(0, COLS[1][p])], lsem.at[6 + p]))
     for copy in mine:
         copy.start()
     pl.semaphore_wait(barrier, len(greet) + 1)
@@ -65,9 +64,10 @@
             for p in range(3):
                 peer, _ = axis_peer(p, d)
                 outgoing.append(pltpu.make_async_remote_copy(
-                    src.at[:, pl.ds(OFF[p], COLS[p])], dst.at[p, c[p], :, pl.ds(0, COLS[p])],
+                    src.at[:, pl.ds(OFF[k][p], COLS[k][p])], dst.at[p, c[p], :, pl.ds(0, COLS[k][p])],
                     bc_s.at[k, p, d - 1], bc_r.at[k, p, d - 1], device_id=peer, device_id_type=MESH))
-    for copy in outgoing:
+    first = len(outgoing) - 6
+    for copy in outgoing[:first]:
         copy.start()
     for copy in weights:
         copy.start()
@@ -79,14 +79,14 @@
             device_id=axis_peer(p, d)[0], device_id_type=MESH)
 
     def bc_in(k, p, d):
-        block = (t_tok, t_cot)[k].at[p, lax.rem(c[p] - d + SIDE, SIDE), :, pl.ds(0, COLS[p])]
+        block = (t_tok, t_cot)[k].at[p, lax.rem(c[p] - d + SIDE, SIDE), :, pl.ds(0, COLS[k][p])]
         return pltpu.make_async_remote_copy(
             block, block, bc_s.at[k, p, d - 1], bc_r.at[k, p, d - 1], device_id=axis_peer(p, d)[0], device_id_type=MESH)
 
     def half(k, p, d, back):
         v = lax.rem(c[p] - (2 if back else d) + SIDE, SIDE)
         i = d // 2
-        block = (t_tok, t_cot)[k].at[p, v, pl.ds(i * 64, 64), pl.ds(0, COLS[p])]
+        block = (t_tok, t_cot)[k].at[p, v, pl.ds(i * 64, 64), pl.ds(0, COLS[k][p])]
         return pltpu.make_async_remote_copy(
             block, block, hf_s.at[k, p, i], hf_r.at[k, p, i], device_id=axis_peer(p, d)[0], device_id_type=MESH)
 
@@ -125,7 +125,7 @@
         return jnp.concatenate(blocks, axis=0).astype(BF)
 
     def pick(k, p, d):
-        n = COLS[p]
+        n = COLS[k][p]
         v = lax.rem(c[p] - d + SIDE, SIDE)
         main_mask(p, v, k == 1)
         rows = pl.ds(pl.multiple_of(v * MAIN, MAIN), MAIN)
@@ -133,7 +133,7 @@
         FROM[k][p, :, rows, 0:n] = got.reshape(PLANE, MAIN, n)
 
     def pick_extra(k, p):
-        n = COLS[p]
+        n = COLS[k][p]
         got = jnp.zeros((PLANE * SIDE * EXTRA, n), F32)
         for v in range(SIDE):
             got += jnp.dot(extra_mask(p, v, k == 1), SPREAD[k][p, v, :, 0:n], preferred_element_type=F32)
@@ -141,14 +141,14 @@
             FROM[k][p, uw, SIDE * MAIN:ROWS, 0:n] = got[uw * 8:uw * 8 + 8].astype(BF)
 
     def land(k, p, at):
-        n = pl.ds(0, COLS[p])
+        n = pl.ds(0, COLS[k][p])
         if k == 2 and p == 0:
             return r_last.at[at, :, n]
         return (x_hbm, c_hbm, r_hbm)[k].at[p, at, :, n]
 
 
     def hop(k, p, a, b, first):
-        n = pl.ds(0, COLS[p])
+        n = pl.ds(0, COLS[k][p])
         u, w = near(p, a, b)
         src = FROM[k].at[p, u * SIDE + w, :, n]
         if first:
@@ -160,7 +160,7 @@
             src, dst, pl_s.at[k, p, a * SIDE + b], sem, device_id=to, device_id_type=MESH)
 
     def relay(k, p, a, b):
-        n = pl.ds(0, COLS[p])
+        n = pl.ds(0, COLS[k][p])
         i = (a - 1) * 3 + b - 1
         u, _ = near(p, -a, 0)
         _, w = near(p, 0, b)
@@ -171,7 +171,7 @@
         relay_copy(k, p, a, b, u, to).start()
 
     def relay_copy(k, p, a, b, u, to):
-        n = pl.ds(0, COLS[p])
+        n = pl.ds(0, COLS[k][p])
         i = (a - 1) * 3 + b - 1
         return pltpu.make_async_remote_copy(
             y_hbm.at[k, p, i, :, n], land(k, p, u * SIDE + c[OTHER[p][1]]),
@@ -185,13 +185,14 @@
         lax.fori_loop(start, stop, step, 0)
 
     def keep(k, p):
-        n = pl.ds(0, COLS[p])
+        n = pl.ds(0, COLS[k][p])
         return pltpu.make_async_copy(FROM[k].at[p, own[p], :, n], land(k, p, own[p]), ssem.at[k, p])
 
-    def launch(k):
+    def launch_far(k, p):
         for i in range(9):
-            for p in range(3):
-                hop(k, p, i // 3 + 1, i % 3 + 1, True).start()
+            hop(k, p, i // 3 + 1, i % 3 + 1, True).start()
+
+    def launch_near(k):
         for a in (2, 1, 3):
             for p in range(3):
                 hop(k, p, 0, a, False).start()
@@ -199,30 +200,40 @@
         for p in range(3):
             keep(k, p).start()
 
+    def launch(k):
+        for i in range(9):
+            for p in range(3):
+                hop(k, p, i // 3 + 1, i % 3 + 1, True).start()
+        launch_near(k)
+
     def far(k, p):
         for d in (1, 3):
             half(k, p, d, True).wait_recv()
 
+    cot_out = outgoing[first:]
     forward(0)
+    for copy in cot_out:
+        copy.start()
     for p in range(3):
         mine[3 * p + 1].wait()
         for d in (0, 1, 3):
             pick(0, p, d)
-    forward(1)
     for p in range(3):
         far(0, p)
         pick(0, p, 2)
         pick_extra(0, p)
-    launch(0)
+        launch_far(0, p)
+    launch_near(0)
+    forward(1)
     for p in range(3):
         mine[3 * p + 2].wait()
         for d in (0, 1, 3):
             pick(1, p, d)
+    relays(0, 0, 9)
     for p in range(3):
         far(1, p)
         pick(1, p, 2)
         pick_extra(1, p)
-    relays(0, 0, 9)
     launch(1)
 
     def arrived(k, p):
@@ -238,7 +249,7 @@
 
     def sent(k, p):
         def step(i, carry):
-            n = pl.ds(0, COLS[p])
+            n = pl.ds(0, COLS[k][p])
             u, w = near(p, i // SIDE, i % SIDE)
             block = FROM[k].at[p, u * SIDE + w, :, n]
             pltpu.make_async_remote_copy(block, block, pl_s.at[k, p, i], pl_r.at[k, p, i],
@@ -261,15 +272,15 @@
             z, x = q // SIDE, q % SIDE
             rows = pl.ds(q * MAIN, MAIN)
             pltpu.make_async_copy(
-                src.at[0, q, pl.ds(pl.multiple_of(g * MAIN, MAIN), MAIN), :],
-                stage.at[slot, rows, pl.ds(OFF[0], WIDE)], esem.at[slot]).start()
+                src.at[0, q, pl.ds(pl.multiple_of(g * MAIN, MAIN), MAIN), pl.ds(0, COLS[k][0])],
+                stage.at[slot, rows, pl.ds(OFF[k][0], COLS[k][0])], esem.at[slot]).start()
             pltpu.make_async_copy(
-                src.at[1, x * SIDE + g, pl.ds(z * MAIN, MAIN), :],
-                stage.at[slot, rows, pl.ds(OFF[1], WIDE)], esem.at[slot]).start()
-            n = COLS[2]
+                src.at[1, x * SIDE + g, pl.ds(z * MAIN, MAIN), pl.ds(0, COLS[k][1])],
+                stage.at[slot, rows, pl.ds(OFF[k][1], COLS[k][1])], esem.at[slot]).start()
+            n = COLS[k][2]
             pltpu.make_async_copy(
                 src.at[2, g * SIDE + z, pl.ds(x * MAIN, MAIN), pl.ds(0, n)],
-                stage.at[slot, rows, pl.ds(OFF[2], n)], esem.at[slot]).start()
+                stage.at[slot, rows, pl.ds(OFF[k][2], n)], esem.at[slot]).start()
 
     def stage_wait(k, slot):
         pltpu.make_async_copy(stage.at[slot], stage.at[slot], esem.at[slot]).wait()
@@ -279,8 +290,8 @@
         for p in range(3):
             for q in range(PLANE):
                 pltpu.make_async_copy(
-                    src.at[p, q, pl.ds(SIDE * MAIN, 8), pl.ds(0, COLS[p])],
-                    ext.at[pl.ds(q * 8, 8), pl.ds(OFF[p], COLS[p])], esem.at[2]).start()
+                    src.at[p, q, pl.ds(SIDE * MAIN, 8), pl.ds(0, COLS[k][p])],
+                    ext.at[pl.ds(q * 8, 8), pl.ds(OFF[k][p], COLS[k][p])], esem.at[2]).start()
         pltpu.make_async_copy(ext, ext, esem.at[2]).wait()
 
     ra = lax.broadcasted_iota(jnp.int32, (128, 128), 0)
@@ -299,7 +310,7 @@
     def extra_into_stage(k, slot):
         stage_extra(k)
         for p in range(3):
-            cols = slice(OFF[p], OFF[p] + COLS[p])
+            cols = slice(OFF[k][p], OFF[k][p] + COLS[k][p])
             block = ext[:, cols]
             if p < 2:
                 block = jnp.dot(to_canon(p), block, preferred_element_type=F32).astype(BF)
@@ -317,7 +328,7 @@
         lax.fori_loop(0, FF // 256, tile, 0)
 
     def down(m, p):
-        return jnp.dot(hid[0:m, :], wd[:, OFF[p]:OFF[p] + COLS[p]], preferred_element_type=F32).astype(BF)
+        return jnp.dot(hid[0:m, :], wd[:, OFF[2][p]:OFF[2][p] + COLS[2][p]], preferred_element_type=F32).astype(BF)
 
     for p in range(3):
         arrived(0, p)
@@ -333,7 +344,7 @@
         if p < 2:
             out = jnp.dot(from_canon(p), out, preferred_element_type=F32).astype(BF)
         for q in range(PLANE):
-            buf_a[p, q, SIDE * MAIN:ROWS, 0:COLS[p]] = out[q * 8:q * 8 + 8]
+            buf_a[p, q, SIDE * MAIN:ROWS, 0:COLS[2][p]] = out[q * 8:q * 8 + 8]
 
     def token_group(i, carry):
         slot = i % 2
@@ -346,54 +357,21 @@
 
         expert(slot, 256, pl.multiple_of(g * 256, 256))
         out = down(256, 2)
-        buf_a[2, pl.ds(g * SIDE, SIDE), 0:SIDE * MAIN, 0:COLS[2]] = out.reshape(SIDE, SIDE * MAIN, COLS[2])
+        buf_a[2, pl.ds(g * SIDE, SIDE), 0:SIDE * MAIN, 0:COLS[2][2]] = out.reshape(SIDE, SIDE * MAIN, COLS[2][2])
         out = down(256, 1)
         for z in range(SIDE):
             for x in range(SIDE):
                 r = (z * SIDE + x) * MAIN
                 buf_a[1, x * SIDE + g, z * MAIN:(z + 1) * MAIN, :] = out[r:r + MAIN]
-        @pl.when(i == 0)
-        def _():
-            for a in (2, 1, 3):
-                hop(2, 1, a, 0, False).start()
-                hop(2, 2, 0, a, False).start()
-
-        @pl.when(i > 0)
-        def _():
-            for a in (1, 2, 3):
-                hop(2, 1, a, i, True).start()
-                hop(2, 2, i, a, True).start()
-            hop(2, 1, 0, i, False).start()
-            hop(2, 2, i, 0, False).start()
-
         out = down(256, 0)
-        buf_a[0, :, pl.ds(pl.multiple_of(g * MAIN, MAIN), MAIN), :] = out.reshape(PLANE, MAIN, COLS[0])
+        buf_a[0, :, pl.ds(pl.multiple_of(g * MAIN, MAIN), MAIN), 0:COLS[2][0]] = out.reshape(PLANE, MAIN, COLS[2][0])
         relays(1, 2 * i, 2 * i + 2)
         return carry
 
     lax.fori_loop(0, SIDE, token_group, 0)
-    for i in range(9):
-        hop(2, 0, i // 3 + 1, i % 3 + 1, True).start()
-    for a in (2, 1, 3):
-        hop(2, 0, 0, a, False).start()
-        hop(2, 0, a, 0, False).start()
-    for p in range(3):
-        keep(2, p).start()
+    launch(2)
     relays(1, 8, 9)
-
-    def relay_returns(i, carry):
-        for a in (1, 2, 3):
-            relay(2, 1, a, i)
-            relay(2, 2, i, a)
-        return carry
-
-    lax.fori_loop(1, SIDE, relay_returns, 0)
-
-    def relay_last(i, carry):
-        relay(2, 0, i // 3 + 1, i % 3 + 1)
-        return carry
-
-    lax.fori_loop(0, 9, relay_last, 0)
+    relays(2, 0, 9)
 
     for p in range(3):
         arrived(1, p)
@@ -433,49 +411,82 @@
         sent(1, p)
     for copy in outgoing:
         copy.wait_send()
-    red_out = []
-    for p in (2, 1, 0):
-        n = COLS[p]
-        arrived(2, p)
-        if p == 0:
-            block = r_last
-            left = jnp.concatenate([r_last[q, SIDE * MAIN:ROWS, :].astype(F32) for q in range(PLANE)], axis=0)
-            ext[:, OFF[p]:OFF[p] + n] = left.astype(BF)
-        else:
-            block = buf_b.at[p]
-            whole = pltpu.make_async_copy(r_hbm.at[p, :, :, pl.ds(0, n)], buf_b.at[p, :, :, pl.ds(0, n)], ssem.at[1, p])
-            whole.start()
-            for q in range(PLANE):
-                pltpu.make_async_copy(
-                    r_hbm.at[p, q, pl.ds(SIDE * MAIN, 8), pl.ds(0, n)],
-                    ext.at[pl.ds(q * 8, 8), pl.ds(OFF[p], n)], esem.at[2]).start()
-            e = ext.at[:, pl.ds(OFF[p], n)]
-            pltpu.make_async_copy(e, e, esem.at[2]).wait()
-            whole.wait()
-        for d in (2, 1, 3, 0):
-            peer, v = axis_peer(p, d)
-            main_mask(p, v, True)
-            rows = block[:, pl.ds(pl.multiple_of(v * MAIN, MAIN), MAIN), 0:n].reshape(PLANE * MAIN, n)
-            total = lax.dot_general(pm[...], rows, (((0,), (0,)), ((), ())), preferred_element_type=F32)
-            total += lax.dot_general(extra_mask(p, v, True), ext[:, OFF[p]:OFF[p] + n], (((0,), (0,)), ((), ())),
-                                     preferred_element_type=F32)
-            t_tok[p, d, :, 0:n] = total.astype(BF)
-            src, dst = t_tok.at[p, d, :, pl.ds(0, n)], part.at[d, :, pl.ds(OFF[p], n)]
-            if d == 0:
-                copy = pltpu.make_async_copy(src, dst, lsem.at[p])
-            else:
-                copy = pltpu.make_async_remote_copy(
-                    src, dst, red_s.at[p, d - 1], red_r.at[p, d - 1], device_id=peer, device_id_type=MESH)
-            copy.start()
-            red_out.append(copy)
+    def fetch(p):
+        n = COLS[2][p]
+        whole = pltpu.make_async_copy(r_hbm.at[p, :, :, pl.ds(0, n)], buf_b.at[p, :, :, pl.ds(0, n)], ssem.at[1, p])
+        whole.start()
+        for q in range(PLANE):
+            pltpu.make_async_copy(
+                r_hbm.at[p, q, pl.ds(SIDE * MAIN, 8), pl.ds(0, n)],
+                ext.at[pl.ds(q * 8, 8), pl.ds(OFF[2][p], n)], esem.at[p - 1]).start()
+        return whole
+
+    def weighted(p, d):
+        n = COLS[2][p]
+        v = lax.rem(c[p] + d, SIDE)
+        block = r_last if p == 0 else buf_b.at[p]
+        main_mask(p, v, True)
+        rows = block[:, pl.ds(pl.multiple_of(v * MAIN, MAIN), MAIN), 0:n].reshape(PLANE * MAIN, n)
+        total = lax.dot_general(pm[...], rows, (((0,), (0,)), ((), ())), preferred_element_type=F32)
+        return total + lax.dot_general(extra_mask(p, v, True), ext[:, OFF[2][p]:OFF[2][p] + n], (((0,), (0,)), ((), ())),
+                                       preferred_element_type=F32)
+
+    def side_sum(p, i):
+        n = pl.ds(0, COLS[2][p])
+        return pltpu.make_async_remote_copy(
+            t_tok.at[p, 2, pl.ds(i * 64, 64), n], side.at[p, i, :, n], sd_s.at[p, i], sd_r.at[p, i],
+            device_id=axis_peer(p, 2 * i + 1)[0], device_id_type=MESH)
+
+    def last_sum(p, i):
+        n = COLS[2][p]
+        d = 2 * i + 1
+        return pltpu.make_async_remote_copy(
+            t_tok.at[p, d, :, pl.ds(0, n)], part.at[1 + i, :, pl.ds(OFF[2][p], n)], red_s.at[p, i], red_r.at[p, i],
+            device_id=axis_peer(p, d)[0], device_id_type=MESH)
+
+    arrived(2, 2)
+    loads = {2: fetch(2)}
+    arrived(2, 1)
+    loads[1] = fetch(1)
+    arrived(2, 0)
+    left = jnp.concatenate([r_last[q, SIDE * MAIN:ROWS, 0:COLS[2][0]].astype(F32) for q in range(PLANE)], axis=0)
+    ext[:, 0:COLS[2][0]] = left.astype(BF)
+    for p in (0, 2, 1):
+        if p:
+            e = ext.at[:, pl.ds(OFF[2][p], COLS[2][p])]
+            pltpu.make_async_copy(e, e, esem.at[p - 1]).wait()
+            loads[p].wait()
+        t_tok[p, 2, :, 0:COLS[2][p]] = weighted(p, 2).astype(BF)
+        for i in range(2):
+            side_sum(p, i).start()
+    mine = []
+    for p in (0, 2, 1):
+        n = COLS[2][p]
+        for i in range(2):
+            total = weighted(p, 2 * i + 1)
+            side_sum(p, i).wait_recv()
+            added = total[i * 64:i * 64 + 64] + side[p, i, :, 0:n].astype(F32)
+            t_tok[p, 2 * i + 1, i * 64:i * 64 + 64, 0:n] = added.astype(BF)
+            t_tok[p, 2 * i + 1, 64 - i * 64:128 - i * 64, 0:n] = total[64 - i * 64:128 - i * 64].astype(BF)
+            last_sum(p, i).start()
+    for p in (0, 2, 1):
+        n = COLS[2][p]
+        t_tok[p, 0, :, 0:n] = weighted(p, 0).astype(BF)
+        copy = pltpu.make_async_copy(t_tok.at[p, 0, :, pl.ds(0, n)], part.at[0, :, pl.ds(OFF[2][p], n)], lsem.at[p])
+        copy.start()
+        mine.append(copy)
     pair.wait()
     grad[...] = acc[0:1, :] + grecv[0:1, :]
     for p in range(3):
         sent(2, p)
         for k in range(3):
             relayed(k, p)
-    for copy in red_out:
+    for copy in mine:
         copy.wait()
+    for p in range(3):
+        for i in range(2):
+            side_sum(p, i).wait_send()
+            last_sum(p, i).wait()
 
 
 def shards(tokens, expert_ids, route_weights, cotangent, w_gate, w_up, w_down, ia3_scale):
@@ -500,7 +511,7 @@
     dma = pltpu.SemaphoreType.DMA
     out = pl.pallas_call(
         kernel,
-        out_shape=[jax.ShapeDtypeStruct((SIDE, TOK, D), BF), jax.ShapeDtypeStruct((1, FF), F32), land, land, land,
+        out_shape=[jax.ShapeDtypeStruct((3, TOK, D), BF), jax.ShapeDtypeStruct((1, FF), F32), land, land, land,
                    jax.ShapeDtypeStruct((3, 3, 9, ROWS, WIDE), BF)],
         in_specs=[hbm] * 6 + [vmem],
         out_specs=[hbm, vmem, hbm, hbm, hbm, hbm],
@@ -518,13 +529,14 @@
             pltpu.VMEM((256, FF), BF),
             pltpu.VMEM((2, 256, D), BF),
             pltpu.VMEM((128, D), BF),
+            pltpu.VMEM((3, 2, 64, WIDE), BF),
             pltpu.VMEM((256, TOK), BF),
             pltpu.VMEM((8, FF), F32),
             pltpu.VMEM((8, FF), F32),
             pltpu.VMEM((8, FF), F32),
             dma((3,)), dma((9,)), dma((3, 3)), dma((3,)),
             dma((3, 3)), dma((3, 3)), dma((2, 3, 3)), dma((2, 3, 3)), dma((2, 3, 2)), dma((2, 3, 2)),
-            dma((3, 3, PLANE)), dma((3, 3, PLANE)), dma((3, 3, 9)), dma((3, 3, 9)), dma((3, 3)), dma((3, 3)), dma(()), dma(()),
+            dma((3, 3, PLANE)), dma((3, 3, PLANE)), dma((3, 3, 9)), dma((3, 3, 9)), dma((3, 2)), dma((3, 2)), dma((3, 2)), dma((3, 2)), dma(()), dma(()),
         ],
         compiler_params=pltpu.CompilerParams(collective_id=0, has_side_effects=True, vmem_limit_bytes=67043328),
     )(tokens, cotangent, cc, w_gate, w_up, w_down, ia3_scale)

time: 276 us -> 267 us (0.967)
  Pallas kernels: 265 us -> 259 us
    pallas_call x1, Pallas kernels: 265 us -> 259 us  [shards(): pl.pallas_call(kernel, out_shape=[jax.ShapeDtypeStruct((3, TOK, D), BF),...]
where the time goes in v4:
time: 267 us
  Pallas kernels  259 us (97%)
  other arithmetic  5.87 us (2%)
    pallas_call x1, Pallas kernels, shards(): pl.pallas_call(kernel, out_shape=[jax.ShapeDtypeStruct((3, TOK, D), BF),...  259 us

profile of v4, /device:TPU:0, one launch (start us, length us, event | category | flops | bytes accessed | tf_op | source)
XLA Modules:
  0.0 267.0 jit_solution(8866151020307624695)
XLA Ops:
  0.6 0.7 convert_bitcast_fusion
  1.3 0.7 convert_reduce_fusion
  2.1 0.1 convolution_select_fusion
  2.3 0.7 pad_maximum_fusion.cc
  3.0 259.1 %shard_map.95 = (bf16[3,128,4096]{2,1,0:T(8,128)(2,1)}, f32[1,768]{1,0:T(1,128)}, bf16[3,16,72,1408]{3,2,1,0:T(8,128)(2,1)}, bf16[3,16,72,1408]{3,2,1,0:T(8,128)...) custom-call(bf16[128,4096]{1,0:T(8,128)(2,1)} %tok.1, bf16[128,4096]{1,0:T(8,128)(2,1)} %cot.1, ...), custom_call_target="tpu_custom_call" | custom-call | tf_op jit(solution)/shard_map/pallas_call | solution.py:512
  262.1 3.7 %reduce_sum.32 = bf16[128,4096]{1,0:T(8,128)(2,1)} reduce(bf16[3,128,4096]{2,1,0:T(8,128)(2,1)} %get-tuple-element.4, bf16[]{:T(256)} %constant.6.clone.1), dimensions={0}, to_apply=%region_2.3 | reduce | flops 1048576 | bytes 4194306 | tf_op jit(solution)/shard_map/reduce_sum | solution.py:543
  265.8 1.2 copy.20
  (4 shorter events, 0.1 us)

commit v5 on v4

--- a/solution.py
+++ b/solution.py
@@ -18,7 +18,7 @@
 
 
 def kernel(tok, cot, cc, wg_hbm, wu_hbm, wd_hbm, scale, part, grad, x_hbm, c_hbm, r_hbm, y_hbm,
-           t_tok, t_cot, buf_a, buf_b, r_last, ids, wg, wu, wd, act, hid, stage, ext, side, pm, acc, gsend, grecv,
+           t_tok, t_cot, buf_a, buf_b, r_last, ids, wg, wu, wd, act, hid, stage, ext, side, mix, pm, acc, gsend, grecv,
            wsem, lsem, ssem, esem, id_s, id_r, bc_s, bc_r, hf_s, hf_r, pl_s, pl_r, y_s, y_r, sd_s, sd_r, red_s, red_r, rep_s, rep_r):
     rep = lax.axis_index("rep")
     me = lax.axis_index("exp")
@@ -211,12 +211,14 @@
             half(k, p, d, True).wait_recv()
 
     cot_out = outgoing[first:]
+    for p in range(3):
+        mine[3 * p + 1].wait()
+        pick(0, p, 0)
     forward(0)
     for copy in cot_out:
         copy.start()
     for p in range(3):
-        mine[3 * p + 1].wait()
-        for d in (0, 1, 3):
+        for d in (1, 3):
             pick(0, p, d)
     for p in range(3):
         far(0, p)
@@ -425,11 +427,9 @@
         n = COLS[2][p]
         v = lax.rem(c[p] + d, SIDE)
         block = r_last if p == 0 else buf_b.at[p]
-        main_mask(p, v, True)
         rows = block[:, pl.ds(pl.multiple_of(v * MAIN, MAIN), MAIN), 0:n].reshape(PLANE * MAIN, n)
-        total = lax.dot_general(pm[...], rows, (((0,), (0,)), ((), ())), preferred_element_type=F32)
-        return total + lax.dot_general(extra_mask(p, v, True), ext[:, OFF[2][p]:OFF[2][p] + n], (((0,), (0,)), ((), ())),
-                                       preferred_element_type=F32)
+        total = jnp.dot(mix[p, d, :, 0:256], rows, preferred_element_type=F32)
+        return total + jnp.dot(mix[p, d, :, 256:384], ext[:, OFF[2][p]:OFF[2][p] + n], preferred_element_type=F32)
 
     def side_sum(p, i):
         n = pl.ds(0, COLS[2][p])
@@ -444,6 +444,12 @@
             t_tok.at[p, d, :, pl.ds(0, n)], part.at[1 + i, :, pl.ds(OFF[2][p], n)], red_s.at[p, i], red_r.at[p, i],
             device_id=axis_peer(p, d)[0], device_id_type=MESH)
 
+    for p in range(3):
+        for d in range(SIDE):
+            v = lax.rem(c[p] + d, SIDE)
+            main_mask(p, v, True)
+            mix[p, d, :, 0:256] = pm[...].astype(F32).T.astype(BF)
+            mix[p, d, :, 256:384] = extra_mask(p, v, True).astype(F32).T.astype(BF)
     arrived(2, 2)
     loads = {2: fetch(2)}
     arrived(2, 1)
@@ -530,6 +536,7 @@
             pltpu.VMEM((2, 256, D), BF),
             pltpu.VMEM((128, D), BF),
             pltpu.VMEM((3, 2, 64, WIDE), BF),
+            pltpu.VMEM((3, SIDE, TOK, 384), BF),
             pltpu.VMEM((256, TOK), BF),
             pltpu.VMEM((8, FF), F32),
             pltpu.VMEM((8, FF), F32),

time: 267 us -> 267 us (level)
  no operation moved by 1% of the time
where the time goes in v5:
time: 267 us
  Pallas kernels  259 us (97%)
  other arithmetic  5.87 us (2%)
    pallas_call x1, Pallas kernels, shards(): pl.pallas_call(kernel, out_shape=[jax.ShapeDtypeStruct((3, TOK, D), BF),...  259 us

profile of v5, /device:TPU:0, one launch (start us, length us, event | category | flops | bytes accessed | tf_op | source)
XLA Modules:
  0.0 266.9 jit_solution(8723451520265695982)
XLA Ops:
  0.6 0.7 convert_bitcast_fusion
  1.3 0.7 convert_reduce_fusion
  2.1 0.1 convolution_select_fusion
  2.3 0.7 pad_maximum_fusion.cc
  3.0 258.9 %shard_map.95 = (bf16[3,128,4096]{2,1,0:T(8,128)(2,1)}, f32[1,768]{1,0:T(1,128)}, bf16[3,16,72,1408]{3,2,1,0:T(8,128)(2,1)}, bf16[3,16,72,1408]{3,2,1,0:T(8,128)...) custom-call(bf16[128,4096]{1,0:T(8,128)(2,1)} %tok.1, bf16[128,4096]{1,0:T(8,128)(2,1)} %cot.1, ...), custom_call_target="tpu_custom_call" | custom-call | tf_op jit(solution)/shard_map/pallas_call | solution.py:518
  261.9 3.7 %reduce_sum.32 = bf16[128,4096]{1,0:T(8,128)(2,1)} reduce(bf16[3,128,4096]{2,1,0:T(8,128)(2,1)} %get-tuple-element.4, bf16[]{:T(256)} %constant.6.clone.1), dimensions={0}, to_apply=%region_2.3 | reduce | flops 1048576 | bytes 4194306 | tf_op jit(solution)/shard_map/reduce_sum | solution.py:550
  265.7 1.2 copy.20
  (4 shorter events, 0.1 us)
